TPU v7x, 32 devices: a whole 2x2x4 slice. The times are simulated.
32 devices in a mesh: ka: 8 (over z, y), row: 4 (over x, core).
Axes of the slice: x: 2, y: 2, z: 4, core: 2. Of those that a mesh axis runs over, the one named last changes fastest.
Arguments:
- occupied: bfloat16 [8, 8, 16384], P('ka', None, 'row'), may hold values from -6 to 6
- empty: bfloat16 [8, 64, 16384], P('ka', None, 'row'), may hold values from -6 to 6
- occ_energy: bfloat16 [8, 8], P('ka'), may hold values from -3 to -0.5
- emp_energy: bfloat16 [8, 64], P('ka'), may hold values from 0.5 to 3
- partner: int32 [2, 8], replicated, may hold values from 0 to 7, as said below
- gvecs: int32 [2, 384, 3], replicated, may hold values from -4 to 4
Outputs:
- polarity: float32 [2, 768, 768], P(None, 'ka', 'row')
Inputs may be any that keep to these rules, and one draw needn't show every extreme that they name: partner[q, k] is the index of k + q_q on the periodic 4 x 2 x 1 grid of k-points, k = (i * 2 + j) + l, where each momentum q_q is a nonzero step along the first dimension only.
All inputs are finite; a program needn't handle non-finite values.
Results may differ from a plain program's by a relative error of at most 0.004.
Values may be sent and summed in bfloat16 or wider, within the bound.
No kernel may reach another device: no remote copies, remote signals or barrier semaphores. Data moves between devices by JAX's collectives and lax.ppermute only.
A program may use at most 64 MiB of HBM per device.

v0:
```python
import functools
import math

import jax
import jax.numpy as jnp
import numpy as np
from jax import lax
from jax.experimental import pallas as pl
from jax.experimental.pallas import tpu as pltpu
from jax.sharding import PartitionSpec as P


GY = 16
GZ = 32
REACH = 4
SHIFTS = 4
LANES = 128

SIDE = 2 * REACH + 1
FACTORS = SIDE
HALF = LANES // 2


def plane_table():
    u = np.arange(HALF)
    h1 = (u + REACH) // SIDE
    h2 = u - SIDE * h1
    y, z = np.divmod(np.arange(GY * GZ), GZ)
    turns = (h1[None, :] * y[:, None] * GZ + h2[None, :] * z[:, None] * GY) % (GY * GZ)
    angle = 2.0 * np.pi * turns / (GY * GZ)
    used = (u <= (SIDE * SIDE) // 2)[None, :]
    whole = np.concatenate([np.cos(angle) * used, np.sin(angle) * used], axis=1).astype(np.float32)
    high = whole.astype(jnp.bfloat16)
    low = (whole - high.astype(np.float32)).astype(jnp.bfloat16)
    return np.concatenate([high, low], axis=1)


def turn_table(grid_x, count):
    middle = count * np.arange(2)[:, None] + (count - 1) / 2
    angle = 2.0 * np.pi * np.arange(1, REACH + 1)[None, :] * middle / grid_x
    return np.concatenate([np.cos(angle), np.sin(angle)], axis=1).astype(np.float32)


def column_index(waves):
    g0, flat = waves[:, 0], waves[:, 1] * SIDE + waves[:, 2]
    u = jnp.abs(flat)
    turn = jnp.where(flat < 0, -1, 1)
    side = jnp.sign(g0)
    cos_row = jnp.abs(g0) * LANES + u
    sin_row = jnp.where(g0 == 0, 0, REACH + jnp.abs(g0)) * LANES + u
    half = waves.shape[0] // 2

    def order(cosine, sine):
        return jnp.concatenate([cosine[:half], sine[:half], cosine[half:], sine[half:]])

    return jnp.stack(
        [
            order(cos_row, sin_row),
            order(sin_row + HALF, cos_row + HALF),
            order(jnp.ones_like(g0), side),
            order(-turn * side, turn),
        ]
    )


def vmem(count):
    return [pl.BlockSpec(memory_space=pltpu.VMEM)] * count


SMEM = pl.BlockSpec(memory_space=pltpu.SMEM)


def room(mebibytes):
    return pltpu.CompilerParams(vmem_limit_bytes=mebibytes << 20)


def prepare_kernel(stride, choices, table, energy, empty, occupied, choice, mine, theirs, sent, partner, level, sems):
    half = mine.shape[0]
    points = mine.shape[1]
    core = lax.axis_index("row") % 2
    parts = (core, 1 - core)
    copies = [
        pltpu.make_async_copy(empty.at[0, pl.ds(pl.multiple_of(part * half, half), half)], to, sems.at[i])
        for i, (part, to) in enumerate(zip(parts, (mine, theirs)))
    ]
    copies.append(pltpu.make_async_copy(occupied.at[0], sent.at[:, pl.ds(0, points)], sems.at[2]))
    small = [pltpu.make_async_copy(table, partner, sems.at[3]), pltpu.make_async_copy(energy, level, sems.at[4])]
    for copy in small + copies:
        copy.start()
    for copy in small:
        copy.wait()
    steps = [jnp.clip(partner[moment, 0] // stride, 1, choices) - 1 for moment in range(2)]
    choice[0, 0] = steps[0] * choices + steps[1]
    states = sent.shape[0]
    square = (states, states)
    here = lax.broadcasted_iota(jnp.int32, square, 0) == lax.broadcasted_iota(jnp.int32, square, 1)
    spread = jnp.where(here, jnp.broadcast_to(level[...].astype(jnp.float32), square), 0.0)
    column = jnp.sum(spread, axis=1, keepdims=True)
    sent[:, points:] = jnp.broadcast_to(column, (states, LANES)).astype(jnp.bfloat16)
    for copy in copies:
        copy.wait()


def prepare(partner, occ_energy, empty, occupied, stride, choices):
    _, bands, points = empty.shape
    states = occupied.shape[1]
    half = jax.ShapeDtypeStruct((bands // 2, points), jnp.bfloat16)
    return pl.pallas_call(
        functools.partial(prepare_kernel, stride, choices),
        out_shape=[
            jax.ShapeDtypeStruct((1, 1), jnp.int32),
            half,
            half,
            jax.ShapeDtypeStruct((states, points + LANES), jnp.bfloat16),
        ],
        in_specs=[pl.BlockSpec(memory_space=pltpu.HBM)] * 4,
        out_specs=[SMEM] + vmem(3),
        scratch_shapes=[
            pltpu.SMEM(partner.shape, partner.dtype),
            pltpu.VMEM(occ_energy.shape, occ_energy.dtype),
            pltpu.SemaphoreType.DMA((5,)),
        ],
        compiler_params=room(4),
        name="prepare",
    )(*[pltpu.with_memory_space_constraint(value, pltpu.HBM) for value in (partner, occ_energy, empty, occupied)])


def settle_kernel(count, *refs):
    for source, to in zip(refs[:count], refs[count:]):
        to[...] = source[...]


def settle(*blocks):
    return pl.pallas_call(
        functools.partial(settle_kernel, len(blocks)),
        out_shape=[jax.ShapeDtypeStruct(block.shape, block.dtype) for block in blocks],
        in_specs=vmem(len(blocks)),
        out_specs=vmem(len(blocks)),
        compiler_params=room(2),
        name="settle",
    )(*blocks)


def transform(emp, occ, plane, wide, density, part, after=None):
    bands, points = emp.shape
    states = occ.shape[0]
    sheet = plane.shape[0]
    count = points // sheet
    tile = 16
    if occ.dtype != jnp.float32:
        wide[...] = occ[:, :points].astype(jnp.float32)
        occ = wide

    def fill(v):
        for step in range(count):
            at = slice(step * sheet, (step + 1) * sheet)
            row = jnp.broadcast_to(occ[v : v + 1, at], (tile, sheet)).astype(jnp.bfloat16)
            for top in range(0, bands, tile):
                density[v % 2, step * bands + top : step * bands + top + tile, :] = row * emp[top : top + tile, at]

    fill(0)
    for v in range(states):
        if v + 1 < states:
            fill(v + 1)
        made = jnp.dot(density[v % 2], plane[...], preferred_element_type=jnp.float32)
        made = made[:, :LANES] + made[:, LANES:]
        for step in range(count):
            part[step, v * bands : (v + 1) * bands, :] = made[step * bands : (step + 1) * bands]
        if after is not None and v > 0:
            after(v - 1)
    if after is not None:
        after(states - 1)


def fold_pair(place, pair, turns, grid_x, near, far, bands, store):
    count = near.shape[0]
    lower = place[0] if pair == 0 else 1 - place[0]
    sign = (1 - 2 * place[1]).astype(jnp.float32)
    turn = {}
    for g in range(1, REACH + 1):
        scale = sign if g % 2 else 1.0
        turn[g] = turns[lower, g - 1] * scale, turns[lower, REACH + g - 1] * scale
    tall = 8

    def weighted(values, weights):
        total = values[0] * weights[0]
        for value, weight in zip(values[1:], weights[1:]):
            total = total + value * weight
        return total

    def after(v):
        for top in range(v * bands, (v + 1) * bands, tall):
            rows = slice(top, top + tall)
            ones = [near[step, rows, :] for step in range(count)]
            twos = [far[step, rows, :] for step in range(count)]
            for odd in (0, 1):
                both = [one - two if odd else one + two for one, two in zip(ones, twos)]
                half = count // 2
                evens = [both[half + i] + both[half - 1 - i] for i in range(half)]
                odds = [both[half + i] - both[half - 1 - i] for i in range(half)]
                if not odd:
                    store(0, rows, functools.reduce(lambda p, q: p + q, evens))
                for g in range(2 - odd, REACH + 1, 2):
                    angles = [2.0 * math.pi * g * (i + 0.5) / grid_x for i in range(half)]
                    even = weighted(evens, [math.cos(t) for t in angles])
                    rest = weighted(odds, [math.sin(t) for t in angles])
                    c, s = turn[g]
                    store(g, rows, even * c - rest * s)
                    store(REACH + g, rows, even * s + rest * c)

    return after


def first_kernel(emp, occ, plane, part, wide, density):
    transform(emp, occ, plane, wide, density, part)


def own_kernel(emp, occ, plane, index, part, matrix, wide, density):
    share = matrix.shape[0] // occ.shape[0]
    signs = index[2:4, :].astype(jnp.float32)

    def after(v):
        shape = (share, matrix.shape[1])
        rows = lax.broadcasted_iota(jnp.int32, shape, 0) + v * share
        two = jnp.where(rows == index[1:2, :], jnp.broadcast_to(signs[1:2], shape), 0.0)
        one = jnp.where(rows == index[0:1, :], jnp.broadcast_to(signs[0:1], shape), two)
        matrix[v * share : (v + 1) * share, :] = one.astype(jnp.bfloat16)

    transform(emp, occ, plane, wide, density, part, after)


def middle_pair_kernel(grid_x, place, turns, emp, occ, plane, near, total, wide, density, part):
    def store(j, rows, value):
        total[j, rows, :] = value

    transform(emp, occ, plane, wide, density, part, fold_pair(place, 0, turns, grid_x, near, part, emp.shape[0], store))


def last_pair_kernel(
    grid_x, scale, place, turns, emp, occ, plane, near, before, matrix, left, wide, density, part, total, narrow
):
    def store(j, rows, value):
        total[j, rows, :] = before[j, rows, :] + value

    transform(emp, occ, plane, wide, density, part, fold_pair(place, 1, turns, grid_x, near, part, emp.shape[0], store))
    for j in range(FACTORS):
        narrow[:, j * LANES : (j + 1) * LANES] = total[j].astype(jnp.bfloat16)
    proj = jnp.dot(narrow[...], matrix[...], preferred_element_type=jnp.float32)
    left[...] = (proj * scale).astype(jnp.bfloat16)


def scratch_of(emp, states):
    bands, points = emp.shape
    sheet = GY * GZ
    return [
        pltpu.VMEM((states, points), jnp.float32),
        pltpu.VMEM((2, points // sheet * bands, sheet), jnp.bfloat16),
    ]


def project_own(emp, occ, index):
    bands, points = emp.shape
    states = occ.shape[0]
    part_shape = (points // (GY * GZ), bands * states, LANES)
    return pl.pallas_call(
        own_kernel,
        out_shape=[
            jax.ShapeDtypeStruct(part_shape, jnp.float32),
            jax.ShapeDtypeStruct((FACTORS * LANES, index.shape[1]), jnp.bfloat16),
        ],
        in_specs=vmem(4),
        out_specs=vmem(2),
        scratch_shapes=scratch_of(emp, states),
        compiler_params=room(8),
        name="own",
    )(emp, occ, jnp.asarray(plane_table()), index)


def project(part_own, matrix, blocks, place, grid_x, scale):
    (core, x, far) = blocks
    bands, points = core[0].shape
    states = core[1].shape[0]
    pairs = bands * states
    count = points // (GY * GZ)
    columns = matrix.shape[1]
    plane = jnp.asarray(plane_table())
    turns = jnp.asarray(turn_table(grid_x, count))
    part_shape = (count, pairs, LANES)
    total_shape = (FACTORS, pairs, LANES)
    scratch = scratch_of(core[0], states)
    part = pltpu.VMEM(part_shape, jnp.float32)
    part_core = pl.pallas_call(
        first_kernel,
        out_shape=jax.ShapeDtypeStruct(part_shape, jnp.float32),
        in_specs=vmem(3),
        out_specs=vmem(1)[0],
        scratch_shapes=scratch,
        compiler_params=room(6),
        name="core",
    )(*core, plane)
    total = pl.pallas_call(
        functools.partial(middle_pair_kernel, grid_x),
        out_shape=jax.ShapeDtypeStruct(total_shape, jnp.float32),
        in_specs=[SMEM, SMEM] + vmem(4),
        out_specs=vmem(1)[0],
        scratch_shapes=scratch + [part],
        compiler_params=room(8),
        name="pair",
    )(place, turns, *x, plane, part_own)
    return pl.pallas_call(
        functools.partial(last_pair_kernel, grid_x, scale),
        out_shape=jax.ShapeDtypeStruct((pairs, columns), jnp.bfloat16),
        in_specs=[SMEM, SMEM] + vmem(6),
        out_specs=vmem(1)[0],
        scratch_shapes=scratch
        + [part, pltpu.VMEM(total_shape, jnp.float32), pltpu.VMEM((pairs, FACTORS * LANES), jnp.bfloat16)],
        compiler_params=room(14),
        name="last",
    )(place, turns, *far, plane, part_core, total, matrix)


def gram_of(core, values, weights):
    width = values.shape[1] // 2
    at = pl.multiple_of(core * width, LANES)
    right = [
        (values[:, pl.ds(at + tile * LANES, LANES)].astype(jnp.float32) * weights[...]).astype(jnp.bfloat16)
        for tile in range(width // LANES)
    ]
    return lax.dot_general(
        values[...], jnp.concatenate(right, axis=1), (((0,), (0,)), ((), ())), preferred_element_type=jnp.float32
    )


def gram_own_kernel(place, own, w_own, gram):
    gram[...] = gram_of(place[0], own, w_own)


def roll_half(value):
    return pltpu.roll(value, value.shape[1] // 2, 1)


def gram_kernel(place, first, other, w_other, keep, to_y, to_x, to_xy, gram):
    core, x, y = place[0], place[1], place[2]
    gram[...] = first[...] + gram_of(core, other, w_other)
    rows = gram.shape[0] // 8
    order = (0, 2, 1, 3)
    low = lax.broadcasted_iota(jnp.int32, (rows, gram.shape[1]), 1) < gram.shape[1] // 2

    def quadrant(way, zl):
        lower = gram[pl.ds(pl.multiple_of(order[zl] * 2 * rows + way * rows, 8), rows), :]
        upper = gram[pl.ds(pl.multiple_of(order[2 + zl] * 2 * rows + way * rows, 8), rows), :]
        return jnp.where(low, lower, roll_half(upper)), jnp.where(low, roll_half(lower), upper)

    for zl in range(2):
        at = slice(zl * rows, (zl + 1) * rows)
        for way, near, far in ((y, keep, to_x), (1 - y, to_y, to_xy)):
            zero, one = quadrant(way, zl)
            near[at, :] = jnp.where(x == 0, zero, one).astype(near.dtype)
            far[at, :] = jnp.where(x == 0, one, zero).astype(far.dtype)


def middle_kernel(place, keep, from_y, from_x, from_xy, stay, *refs):
    sends, block = refs[:3], refs[3]
    x, z = place[1], place[3]
    rows = keep.shape[0] // 2
    low = lax.broadcasted_iota(jnp.int32, (rows, keep.shape[1]), 1) < keep.shape[1] // 2
    for zl in range(2):
        at = slice(zl * rows, (zl + 1) * rows)
        same = keep[at, :] + from_y[at, :].astype(jnp.float32)
        cross = from_x[at, :].astype(jnp.float32) + from_xy[at, :].astype(jnp.float32)
        zero = jnp.where(x == 0, same, cross)
        one = jnp.where(x == 0, cross, same)
        block[zl] = jnp.where(low, zero, roll_half(one))
        block[2 + zl] = jnp.where(low, roll_half(zero), one)
    stay[...] = block[z]
    for index, send in enumerate(sends):
        send[...] = block[z ^ (index + 1)].astype(send.dtype)


def final_kernel(stay, one, two, three, out):
    total = stay[...] + one[...].astype(jnp.float32)
    total = total + two[...].astype(jnp.float32) + three[...].astype(jnp.float32)
    width = total.shape[1] // 2
    out[0] = total[:, :width]
    out[1] = roll_half(total)[:, :width]


def reduce_near(place, own, other, w_own, w_other):
    wide = own.shape[1]
    kcount, rcount = lax.axis_size("ka"), lax.axis_size("row")
    quarter = (wide // 4, wide // 2)
    first = pl.pallas_call(
        gram_own_kernel,
        out_shape=jax.ShapeDtypeStruct((wide, wide // 2), jnp.float32),
        in_specs=[SMEM] + vmem(2),
        out_specs=vmem(1)[0],
        compiler_params=room(8),
        name="gram_own",
    )(place, own, w_own)
    keep, to_y, to_x, to_xy = pl.pallas_call(
        gram_kernel,
        out_shape=[jax.ShapeDtypeStruct(quarter, d) for d in (jnp.float32, jnp.bfloat16, jnp.bfloat16, jnp.bfloat16)],
        in_specs=[SMEM] + vmem(3),
        out_specs=vmem(4),
        scratch_shapes=[pltpu.VMEM((wide, wide // 2), jnp.float32)],
        compiler_params=room(10),
        name="gram",
    )(place, first, other, w_other)

    def route(dy, dx):
        return [(k * rcount + r, (k ^ dy) * rcount + (r ^ dx)) for k in range(kcount) for r in range(rcount)]

    both = ("ka", "row")
    from_y = lax.ppermute(to_y, both, route(1, 0))
    from_xy = lax.ppermute(to_xy, both, route(1, 2))
    from_x = lax.ppermute(to_x, both, route(0, 2))
    piece = (quarter[0] // 2, quarter[1])
    stay, *sends = pl.pallas_call(
        middle_kernel,
        out_shape=[jax.ShapeDtypeStruct(piece, jnp.float32)] + [jax.ShapeDtypeStruct(piece, jnp.bfloat16)] * 3,
        in_specs=[SMEM] + vmem(4),
        out_specs=vmem(4),
        scratch_shapes=[pltpu.VMEM((4,) + piece, jnp.float32)],
        compiler_params=room(6),
        name="middle",
    )(place, keep, from_y, from_x, from_xy)
    arrived = [lax.ppermute(send, both, route(2 * (m + 1), 0)) for m, send in enumerate(sends)]
    return pl.pallas_call(
        final_kernel,
        out_shape=jax.ShapeDtypeStruct((2, piece[0], piece[1] // 2), jnp.float32),
        in_specs=vmem(4),
        out_specs=vmem(1)[0],
        compiler_params=room(4),
        name="final",
    )(stay, *arrived)


def reduce_far(place, own, other, w_own, w_other):
    kcount = lax.axis_size("ka")
    wide = own.shape[1]
    width = wide // 4
    left = jnp.concatenate([own, other], axis=0)
    weight = jnp.concatenate([w_own[:, :1], w_other[:, :1]], axis=0)
    right = lax.dynamic_slice_in_dim(left, place[0] * 2 * width, 2 * width, 1)
    right = (right.astype(jnp.float32) * weight).astype(jnp.bfloat16)
    gram = lax.dot_general(left, right, (((0,), (0,)), ((), ())), preferred_element_type=jnp.float32)
    gram = gram.reshape(2, 2, width, 2, width).swapaxes(0, 1).reshape(kcount, wide // kcount, 2, width)
    parts = lax.all_to_all(gram.astype(jnp.bfloat16), "ka", 0, 0, tiled=True)
    total = jnp.sum(parts.astype(jnp.float32), axis=0)
    mine = lax.dynamic_index_in_dim(total, place[1], 1, keepdims=False)
    send = lax.dynamic_index_in_dim(total, 1 - place[1], 1, keepdims=False)
    came = lax.ppermute(send, "row", [(r, r ^ 2) for r in range(lax.axis_size("row"))])
    first = place[1] == 0
    return jnp.stack([jnp.where(first, mine, came), jnp.where(first, came, mine)])


def per_device(occupied, empty, occ_energy, emp_energy, partner, gvecs):
    kcount, rcount = lax.axis_size("ka"), lax.axis_size("row")
    assert rcount == 4 and partner.shape[0] == 2
    k, r = lax.axis_index("ka"), lax.axis_index("row")
    x, core = r // 2, r % 2
    points = occupied.shape[2]
    grid_x = points * rcount // (GY * GZ)
    stride = kcount // min(SHIFTS, kcount)
    choices = min(SHIFTS, kcount) - 1
    half = empty.shape[1] // 2
    choice, mine, theirs, sent = prepare(partner, occ_energy, empty, occupied, stride, choices)
    emp_x = lax.ppermute(mine, "row", [(i, i ^ 2) for i in range(rcount)])
    emp_xc = lax.ppermute(theirs, "row", [(i, i ^ 3) for i in range(rcount)])
    emp_c = lax.ppermute(theirs, "row", [(i, i ^ 1) for i in range(rcount)])

    states = occupied.shape[1]

    swap = [(i, i ^ 1) for i in range(rcount)]

    def fetch(shift, operands):
        block, waves = operands

        def route(dx):
            pairs = []
            for i in range(kcount):
                for j in range(rcount):
                    to = j ^ dx
                    pairs.append((i * rcount + j, (i + shift[to // 2] * stride) % kcount * rcount + to))
            return pairs

        both = ("ka", "row")
        near = lax.ppermute(block, both, route(0))
        far = lax.ppermute(block, both, route(2))
        near_c = lax.ppermute(near, "row", swap)
        index = column_index(lax.dynamic_index_in_dim(waves, x, 0, keepdims=False))
        return settle(near, near_c, far, index)

    branches = [functools.partial(fetch, (one + 1, two + 1)) for one in range(choices) for two in range(choices)]
    occ_own, occ_c, occ_x, index = lax.switch(choice[0, 0], branches, (sent, gvecs))
    occ_xc = lax.ppermute(occ_x, "row", swap)

    place = jnp.stack([core, x, k % 2, k // 2]).astype(jnp.int32)
    part_own, matrix = project_own(mine, occ_own, index)
    blocks = ((emp_c, occ_c), (emp_x, occ_x), (emp_xc, occ_xc))
    left = project(part_own, matrix, blocks, place, grid_x, 1.0 / (points * rcount))
    level = occ_own[:, points : points + 1].astype(jnp.float32)

    def weights(which):
        energy = lax.dynamic_slice_in_dim(emp_energy[0], which * half, half, 0).astype(jnp.float32)
        value = 1.0 / (energy[None, :] - level)
        return jnp.broadcast_to(value.reshape(states * half, 1), (states * half, LANES))

    w_own, w_other = weights(core), weights(1 - core)
    other = lax.ppermute(left, "row", swap)
    reduce = reduce_near if kcount == 8 else reduce_far
    return reduce(place, left, other, w_own, w_other)


def solution(mesh):
    placed = (P("ka", None, "row"), P("ka", None, "row"), P("ka", None), P("ka", None), P(), P())

    return jax.shard_map(per_device, mesh=mesh, in_specs=placed, out_specs=P(None, "ka", "row"), check_vma=False)
```

profile of v0, /device:TPU:0, one launch (start us, length us, event | category | flops | bytes accessed | tf_op | source)
XLA Modules:
  0.0 46.8 jit_solution(841023955210208882)
XLA Ops:
  0.0 1.6 %prepare.1 = (s32[1,1]{1,0:T(1,128)}, bf16[32,4096]{1,0:T(8,128)(2,1)S(1)}, bf16[32,4096]{1,0:T(8,128)(2,1)S(1)}, bf16[8,4224]{1,0:T(8,128)(2,1)S(1)}) custom-call(s32[2,8]{1,0:T(2,128)} %table.1, bf16[1,8]{1,0:T(2,128)(2,1)} %energy.1, bf16[1,64,4096]{2,1,0:T(8,128)(2,1)} %empty.1, bf16[1,8,4096]{2,1,0:T(8,128)(2,1)} %occupied.1), custom_call_target="tpu_custom_call" | custom-call | tf_op jit(solution)/shard_map/prepare/pallas_call | solution.py:108
  2.2 2.6 %collective-permute-start.30 = (bf16[32,4096]{1,0:T(8,128)(2,1)S(1)}, bf16[32,4096]{1,0:T(8,128)(2,1)S(1)}, u32[]{:S(2)}, u32[]{:S(2)}) collective-permute-start(bf16[32,4096]{1,0:T(8,128)(2,1)S(1)} %get-tuple-element.109.emp), channel_id=1, source_target_pairs={{0,2},{1,3},{2,0},{3,1},{4,6},{5,7},{6,4},{7,5},{8,10},{9,11},{10,... | collective-permute-start | bytes 786440 | tf_op jit(solution)/shard_map/ppermute | solution.py:468
  5.4 9.3 %conditional.1 = ((bf16[8,4224]{1,0:T(8,128)(2,1)S(1)}, bf16[8,4224]{1,0:T(8,128)(2,1)S(1)}, bf16[8,4224]{1,0:T(8,128)(2,1)S(1)}, s32[4,768]{1,0:T(4,128)S(1)})) conditional(s32[]{:T(128)} %bitcast.139, (bf16[8,4224]{1,0:T(8,128)(2,1)S(1)}, s32[]{:T(128)}, s32[2,384,3]{1,0,2:T(2,128)}) %tuple.32, ...), branch_computations={%region_0.1_spmd, %region_1.2_spmd, %region_2.3_spmd, %region_3.4_... | conditional | flops 26115 | bytes 954026 | solution.py:495
  5.5 1.9 %collective-permute-start.6 = (bf16[8,4224]{1,0:T(8,128)(2,1)S(1)}, bf16[8,4224]{1,0:T(8,128)(2,1)S(1)}, u32[]{:S(2)}, u32[]{:S(2)}) collective-permute-start(bf16[8,4224]{1,0:T(8,128)(2,1)S(1)} %get-tuple-element.65), channel_id=1, source_target_pairs={{0,8},{1,9},{2,26},{3,27},{4,12},{5,13},{6,30},{7,31},{8,16},{9,17... | collective-permute-start | bytes 202760 | tf_op jit(solution)/shard_map/cond/branch_2_fun/ppermute | solution.py:488
  7.3 3.4 %collective-permute-start.8 = (bf16[8,4224]{1,0:T(8,128)(2,1)S(1)}, bf16[8,4224]{1,0:T(8,128)(2,1)S(1)}, u32[]{:S(2)}, u32[]{:S(2)}) collective-permute-start(bf16[8,4224]{1,0:T(8,128)(2,1)S(1)} %get-tuple-element.65), channel_id=1, source_target_pairs={{0,26},{1,27},{2,8},{3,9},{4,30},{5,31},{6,12},{7,13},{8,2},{9,3},... | collective-permute-start | bytes 202760 | tf_op jit(solution)/shard_map/cond/branch_2_fun/ppermute | solution.py:489
  12.2 2.4 %collective-permute-done.8.refs_2_ = bf16[8,4224]{1,0:T(8,128)(2,1)S(1)} collective-permute-done((bf16[8,4224]{1,0:T(8,128)(2,1)S(1)}, bf16[8,4224]{1,0:T(8,128)(2,1)S(1)}, u32[]{:S(2)}, u32[]{:S(2)}) %collective-permute-start.8) | collective-permute-done | bytes 67616 | tf_op jit(solution)/shard_map/cond/branch_2_fun/ppermute | solution.py:489
  14.9 1.4 %own.1 = (f32[8,256,128]{2,1,0:T(8,128)S(1)}, bf16[1152,768]{1,0:T(8,128)(2,1)S(1)}) custom-call(bf16[32,4096]{1,0:T(8,128)(2,1)S(1)} %get-tuple-element.109.emp, bf16[8,4224]{1,0:T(8,128)(2,1)S(1)} %get-tuple-element.110.occ, bf16[512,256]{1,0:T(8,128)(2,1)S(1)} %copy-done, s32[4,768]{1,0:T(4,128)S(1)} %get-tuple-element.111.index), custom_call_target="tpu_custom_call" | custom-call | tf_op jit(solution)/shard_map/own/pallas_call | solution.py:265
  16.3 0.7 %core.1.near = f32[8,256,128]{2,1,0:T(8,128)S(1)} custom-call(bf16[32,4096]{1,0:T(8,128)(2,1)S(1)} %collective-permute-done.29.emp, bf16[8,4224]{1,0:T(8,128)(2,1)S(1)} %get-tuple-element.108.occ, bf16[512,256]{1,0:T(8,128)(2,1)S(1)} %copy-done), custom_call_target="tpu_custom_call" | custom-call | tf_op jit(solution)/shard_map/core/pallas_call | solution.py:292
  17.1 1.7 %pair.1.before = f32[9,256,128]{2,1,0:T(8,128)S(1)} custom-call(s32[4]{0:T(128)S(1)} %pad_add_fusion.45.place, f32[2,8]{1,0:T(2,128)S(1)} %copy-done.1, bf16[32,4096]{1,0:T(8,128)(2,1)S(1)} %collective-permute-done.30.emp, bf16[8,4224]{1,0:T(8,128)(2,1)S(1)} %get-tuple-element.107.occ, bf16[512,256]{1,0:T(8,128)(2,1)S(1)} %copy-done, ...), custom_call_target="tpu_custom_call" | custom-call | tf_op jit(solution)/shard_map/pair/pallas_call | solution.py:301
  18.9 2.6 %last.1.own = bf16[256,768]{1,0:T(8,128)(2,1)S(1)} custom-call(s32[4]{0:T(128)S(1)} %pad_add_fusion.45.place, f32[2,8]{1,0:T(2,128)S(1)} %copy-done.1, bf16[32,4096]{1,0:T(8,128)(2,1)S(1)} %collective-permute-done.27.emp, bf16[8,4224]{1,0:T(8,128)(2,1)S(1)} %collective-permute-done.28.occ, bf16[512,256]{1,0:T(8,128)(2,1)S(1)} %copy-done, ...), custom_call_target="tpu_custom_call" | custom-call | tf_op jit(solution)/shard_map/last/pallas_call | solution.py:310
  22.5 0.9 %gram_own.1.first = f32[768,384]{1,0:T(8,128)S(1)} custom-call(s32[4]{0:T(128)S(1)} %pad_add_fusion.45.place, bf16[256,768]{1,0:T(8,128)(2,1)S(1)} %last.1.own, f32[256,128]{1,0:T(8,128)S(1)} %broadcast_in_dim.78.w_own), custom_call_target="tpu_custom_call" | custom-call | tf_op jit(solution)/shard_map/gram_own/pallas_call | solution.py:392
  23.6 1.3 %gram.1 = (f32[192,384]{1,0:T(8,128)S(1)}, bf16[192,384]{1,0:T(8,128)(2,1)S(1)}, bf16[192,384]{1,0:T(8,128)(2,1)S(1)}, bf16[192,384]{1,0:T(8,128)(2,1)S(1)}) custom-call(s32[4]{0:T(128)S(1)} %pad_add_fusion.45.place, f32[768,384]{1,0:T(8,128)S(1)} %gram_own.1.first, bf16[256,768]{1,0:T(8,128)(2,1)S(1)} %collective-permute-done.31.other, ...), custom_call_target="tpu_custom_call" | custom-call | tf_op jit(solution)/shard_map/gram/pallas_call | solution.py:400
  24.8 1.6 %collective-permute-start.32 = (bf16[192,384]{1,0:T(8,128)(2,1)S(1)}, bf16[192,384]{1,0:T(8,128)(2,1)S(1)}, u32[]{:S(2)}, u32[]{:S(2)}) collective-permute-start(bf16[192,384]{1,0:T(8,128)(2,1)S(1)} %get-tuple-element.115), channel_id=1, source_target_pairs={{0,4},{1,5},{2,6},{3,7},{4,0},{5,1},{6,2},{7,3},{8,12},{9,13},{10,... | collective-permute-start | bytes 442376 | tf_op jit(solution)/shard_map/ppermute | solution.py:414
  26.4 1.4 %collective-permute-start.33 = (bf16[192,384]{1,0:T(8,128)(2,1)S(1)}, bf16[192,384]{1,0:T(8,128)(2,1)S(1)}, u32[]{:S(2)}, u32[]{:S(2)}) collective-permute-start(bf16[192,384]{1,0:T(8,128)(2,1)S(1)} %get-tuple-element.116), channel_id=1, source_target_pairs={{0,2},{1,3},{2,0},{3,1},{4,6},{5,7},{6,4},{7,5},{8,10},{9,11},{10,... | collective-permute-start | bytes 442376 | tf_op jit(solution)/shard_map/ppermute | solution.py:416
  28.4 2.5 %collective-permute-done.32.from_y = bf16[192,384]{1,0:T(8,128)(2,1)S(1)} collective-permute-done((bf16[192,384]{1,0:T(8,128)(2,1)S(1)}, bf16[192,384]{1,0:T(8,128)(2,1)S(1)}, u32[]{:S(2)}, u32[]{:S(2)}) %collective-permute-start.32) | collective-permute-done | bytes 147488 | tf_op jit(solution)/shard_map/ppermute | solution.py:414
  30.9 2.3 %collective-permute-done.33.from_x = bf16[192,384]{1,0:T(8,128)(2,1)S(1)} collective-permute-done((bf16[192,384]{1,0:T(8,128)(2,1)S(1)}, bf16[192,384]{1,0:T(8,128)(2,1)S(1)}, u32[]{:S(2)}, u32[]{:S(2)}) %collective-permute-start.33) | collective-permute-done | bytes 147488 | tf_op jit(solution)/shard_map/ppermute | solution.py:416
  33.2 2.1 %collective-permute-done.34.from_xy = bf16[192,384]{1,0:T(8,128)(2,1)S(1)} collective-permute-done((bf16[192,384]{1,0:T(8,128)(2,1)S(1)}, bf16[192,384]{1,0:T(8,128)(2,1)S(1)}, u32[]{:S(2)}, u32[]{:S(2)}) %collective-permute-start.34) | collective-permute-done | bytes 147488 | tf_op jit(solution)/shard_map/ppermute | solution.py:415
  35.2 0.8 %middle.1 = (f32[96,384]{1,0:T(8,128)S(1)}, bf16[96,384]{1,0:T(8,128)(2,1)S(1)}, bf16[96,384]{1,0:T(8,128)(2,1)S(1)}, bf16[96,384]{1,0:T(8,128)(2,1)S(1)}) custom-call(s32[4]{0:T(128)S(1)} %pad_add_fusion.45.place, f32[192,384]{1,0:T(8,128)S(1)} %get-tuple-element.114.keep, bf16[192,384]{1,0:T(8,128)(2,1)S(1)} %collective-permute-done.32.from_y, ...), custom_call_target="tpu_custom_call" | custom-call | tf_op jit(solution)/shard_map/middle/pallas_call | solution.py:418
  36.1 1.7 %collective-permute-start.35 = (bf16[96,384]{1,0:T(8,128)(2,1)S(1)}, bf16[96,384]{1,0:T(8,128)(2,1)S(1)}, u32[]{:S(2)}, u32[]{:S(2)}) collective-permute-start(bf16[96,384]{1,0:T(8,128)(2,1)S(1)} %get-tuple-element.119), channel_id=1, source_target_pairs={{0,8},{1,9},{2,10},{3,11},{4,12},{5,13},{6,14},{7,15},{8,0},{9,1},... | collective-permute-start | bytes 221192 | tf_op jit(solution)/shard_map/ppermute | solution.py:427
  37.7 2.0 %collective-permute-start.36 = (bf16[96,384]{1,0:T(8,128)(2,1)S(1)}, bf16[96,384]{1,0:T(8,128)(2,1)S(1)}, u32[]{:S(2)}, u32[]{:S(2)}) collective-permute-start(bf16[96,384]{1,0:T(8,128)(2,1)S(1)} %get-tuple-element.120), channel_id=1, source_target_pairs={{0,16},{1,17},{2,18},{3,19},{4,20},{5,21},{6,22},{7,23},{8,24},{9,... | collective-permute-start | bytes 221192 | tf_op jit(solution)/shard_map/ppermute | solution.py:427
  39.7 0.8 %collective-permute-start.37 = (bf16[96,384]{1,0:T(8,128)(2,1)S(1)}, bf16[96,384]{1,0:T(8,128)(2,1)S(1)}, u32[]{:S(2)}, u32[]{:S(2)}) collective-permute-start(bf16[96,384]{1,0:T(8,128)(2,1)S(1)} %get-tuple-element.121), channel_id=1, source_target_pairs={{0,24},{1,25},{2,26},{3,27},{4,28},{5,29},{6,30},{7,31},{8,16},{9,... | collective-permute-start | bytes 221192 | tf_op jit(solution)/shard_map/ppermute | solution.py:427
  40.6 4.1 %collective-permute-done.36.two = bf16[96,384]{1,0:T(8,128)(2,1)S(1)} collective-permute-done((bf16[96,384]{1,0:T(8,128)(2,1)S(1)}, bf16[96,384]{1,0:T(8,128)(2,1)S(1)}, u32[]{:S(2)}, u32[]{:S(2)}) %collective-permute-start.36) | collective-permute-done | bytes 73760 | tf_op jit(solution)/shard_map/ppermute | solution.py:427
  44.8 1.2 %collective-permute-done.37.three = bf16[96,384]{1,0:T(8,128)(2,1)S(1)} collective-permute-done((bf16[96,384]{1,0:T(8,128)(2,1)S(1)}, bf16[96,384]{1,0:T(8,128)(2,1)S(1)}, u32[]{:S(2)}, u32[]{:S(2)}) %collective-permute-start.37) | collective-permute-done | bytes 73760 | tf_op jit(solution)/shard_map/ppermute | solution.py:427
  46.0 0.8 %final.1 = f32[2,96,192]{2,1,0:T(8,128)} custom-call(f32[96,384]{1,0:T(8,128)S(1)} %get-tuple-element.118.stay, bf16[96,384]{1,0:T(8,128)(2,1)S(1)} %collective-permute-done.35.one, bf16[96,384]{1,0:T(8,128)(2,1)S(1)} %collective-permute-done.36.two, bf16[96,384]{1,0:T(8,128)(2,1)S(1)} %collective-permute-done.37.three), custom_call_target="tpu_custom_call" | custom-call | tf_op jit(solution)/shard_map/final/pallas_call | solution.py:428
  (47 shorter events, 4.1 us)
Async XLA Ops:
  1.6 14.7 %collective-permute-start.29 = (bf16[32,4096]{1,0:T(8,128)(2,1)S(1)}, bf16[32,4096]{1,0:T(8,128)(2,1)S(1)}, u32[]{:S(2)}, u32[]{:S(2)}) collective-permute-start(bf16[32,4096]{1,0:T(8,128)(2,1)S(1)} %get-tuple-element.104), channel_id=1, source_target_pairs={{0,1},{1,0},{2,3},{3,2},{4,5},{5,4},{6,7},{7,6},{8,9},{9,8},{10,11... | collective-permute-start | bytes 786440 | tf_op jit(solution)/shard_map/ppermute | solution.py:470
  2.2 14.9 %collective-permute-start.30 = (bf16[32,4096]{1,0:T(8,128)(2,1)S(1)}, bf16[32,4096]{1,0:T(8,128)(2,1)S(1)}, u32[]{:S(2)}, u32[]{:S(2)}) collective-permute-start(bf16[32,4096]{1,0:T(8,128)(2,1)S(1)} %get-tuple-element.109.emp), channel_id=1, source_target_pairs={{0,2},{1,3},{2,0},{3,1},{4,6},{5,7},{6,4},{7,5},{8,10},{9,11},{10,... | collective-permute-start | bytes 786440 | tf_op jit(solution)/shard_map/ppermute | solution.py:468
  4.7 14.1 %collective-permute-start.27 = (bf16[32,4096]{1,0:T(8,128)(2,1)S(1)}, bf16[32,4096]{1,0:T(8,128)(2,1)S(1)}, u32[]{:S(2)}, u32[]{:S(2)}) collective-permute-start(bf16[32,4096]{1,0:T(8,128)(2,1)S(1)} %get-tuple-element.104), channel_id=1, source_target_pairs={{0,3},{1,2},{2,1},{3,0},{4,7},{5,6},{6,5},{7,4},{8,11},{9,10},{10,... | collective-permute-start | bytes 786440 | tf_op jit(solution)/shard_map/ppermute | solution.py:469
  5.4 9.4 %copy-start = (bf16[512,256]{1,0:T(8,128)(2,1)S(1)}, bf16[512,256]{1,0:T(8,128)(2,1)}, u32[]{:S(2)}) copy-start(bf16[512,256]{1,0:T(8,128)(2,1)} %constant.236.clone.plane) | copy-start | bytes 786436
  5.5 6.8 %collective-permute-start.6 = (bf16[8,4224]{1,0:T(8,128)(2,1)S(1)}, bf16[8,4224]{1,0:T(8,128)(2,1)S(1)}, u32[]{:S(2)}, u32[]{:S(2)}) collective-permute-start(bf16[8,4224]{1,0:T(8,128)(2,1)S(1)} %get-tuple-element.65), channel_id=1, source_target_pairs={{0,8},{1,9},{2,26},{3,27},{4,12},{5,13},{6,30},{7,31},{8,16},{9,17... | collective-permute-start | bytes 202760 | tf_op jit(solution)/shard_map/cond/branch_2_fun/ppermute | solution.py:488
  7.3 7.3 %collective-permute-start.8 = (bf16[8,4224]{1,0:T(8,128)(2,1)S(1)}, bf16[8,4224]{1,0:T(8,128)(2,1)S(1)}, u32[]{:S(2)}, u32[]{:S(2)}) collective-permute-start(bf16[8,4224]{1,0:T(8,128)(2,1)S(1)} %get-tuple-element.65), channel_id=1, source_target_pairs={{0,26},{1,27},{2,8},{3,9},{4,30},{5,31},{6,12},{7,13},{8,2},{9,3},... | collective-permute-start | bytes 202760 | tf_op jit(solution)/shard_map/cond/branch_2_fun/ppermute | solution.py:489
  12.2 2.5 %collective-permute-start.7 = (bf16[8,4224]{1,0:T(8,128)(2,1)S(1)}, bf16[8,4224]{1,0:T(8,128)(2,1)S(1)}, u32[]{:S(2)}, u32[]{:S(2)}) collective-permute-start(bf16[8,4224]{1,0:T(8,128)(2,1)S(1)} %collective-permute-done.6.refs_0_), channel_id=1, source_target_pairs={{0,1},{1,0},{2,3},{3,2},{4,5},{5,4},{6,7},{7,6},{8,9},{9,8},{10,11... | collective-permute-start | bytes 202760 | tf_op jit(solution)/shard_map/cond/branch_2_fun/ppermute | solution.py:490
  14.7 2.4 %copy-start.1 = (f32[2,8]{1,0:T(2,128)S(1)}, f32[2,8]{1,0:T(2,128)}, u32[]{:S(2)}) copy-start(f32[2,8]{1,0:T(2,128)} %constant.237.clone.turns) | copy-start | bytes 196
  14.7 4.1 %collective-permute-start.28 = (bf16[8,4224]{1,0:T(8,128)(2,1)S(1)}, bf16[8,4224]{1,0:T(8,128)(2,1)S(1)}, u32[]{:S(2)}, u32[]{:S(2)}) collective-permute-start(bf16[8,4224]{1,0:T(8,128)(2,1)S(1)} %get-tuple-element.107.occ), channel_id=1, source_target_pairs={{0,1},{1,0},{2,3},{3,2},{4,5},{5,4},{6,7},{7,6},{8,9},{9,8},{10,11... | collective-permute-start | bytes 202760 | tf_op jit(solution)/shard_map/ppermute | solution.py:496
  18.9 3.1 %copy-start.2 = (bf16[1,64]{1,0:T(2,128)(2,1)S(1)}, bf16[1,64]{1,0:T(2,128)(2,1)}, u32[]{:S(2)}) copy-start(bf16[1,64]{1,0:T(2,128)(2,1)} %param.21) | copy-start | bytes 388
  21.5 2.0 %collective-permute-start.31 = (bf16[256,768]{1,0:T(8,128)(2,1)S(1)}, bf16[256,768]{1,0:T(8,128)(2,1)S(1)}, u32[]{:S(2)}, u32[]{:S(2)}) collective-permute-start(bf16[256,768]{1,0:T(8,128)(2,1)S(1)} %last.1.own), channel_id=1, source_target_pairs={{0,1},{1,0},{2,3},{3,2},{4,5},{5,4},{6,7},{7,6},{8,9},{9,8},{10,11... | collective-permute-start | bytes 1179656 | tf_op jit(solution)/shard_map/ppermute | solution.py:510
  24.8 6.1 %collective-permute-start.32 = (bf16[192,384]{1,0:T(8,128)(2,1)S(1)}, bf16[192,384]{1,0:T(8,128)(2,1)S(1)}, u32[]{:S(2)}, u32[]{:S(2)}) collective-permute-start(bf16[192,384]{1,0:T(8,128)(2,1)S(1)} %get-tuple-element.115), channel_id=1, source_target_pairs={{0,4},{1,5},{2,6},{3,7},{4,0},{5,1},{6,2},{7,3},{8,12},{9,13},{10,... | collective-permute-start | bytes 442376 | tf_op jit(solution)/shard_map/ppermute | solution.py:414
  26.4 6.7 %collective-permute-start.33 = (bf16[192,384]{1,0:T(8,128)(2,1)S(1)}, bf16[192,384]{1,0:T(8,128)(2,1)S(1)}, u32[]{:S(2)}, u32[]{:S(2)}) collective-permute-start(bf16[192,384]{1,0:T(8,128)(2,1)S(1)} %get-tuple-element.116), channel_id=1, source_target_pairs={{0,2},{1,3},{2,0},{3,1},{4,6},{5,7},{6,4},{7,5},{8,10},{9,11},{10,... | collective-permute-start | bytes 442376 | tf_op jit(solution)/shard_map/ppermute | solution.py:416
  27.8 7.4 %collective-permute-start.34 = (bf16[192,384]{1,0:T(8,128)(2,1)S(1)}, bf16[192,384]{1,0:T(8,128)(2,1)S(1)}, u32[]{:S(2)}, u32[]{:S(2)}) collective-permute-start(bf16[192,384]{1,0:T(8,128)(2,1)S(1)} %get-tuple-element.117), channel_id=1, source_target_pairs={{0,6},{1,7},{2,4},{3,5},{4,2},{5,3},{6,0},{7,1},{8,14},{9,15},{10,... | collective-permute-start | bytes 442376 | tf_op jit(solution)/shard_map/ppermute | solution.py:415
  36.1 4.6 %collective-permute-start.35 = (bf16[96,384]{1,0:T(8,128)(2,1)S(1)}, bf16[96,384]{1,0:T(8,128)(2,1)S(1)}, u32[]{:S(2)}, u32[]{:S(2)}) collective-permute-start(bf16[96,384]{1,0:T(8,128)(2,1)S(1)} %get-tuple-element.119), channel_id=1, source_target_pairs={{0,8},{1,9},{2,10},{3,11},{4,12},{5,13},{6,14},{7,15},{8,0},{9,1},... | collective-permute-start | bytes 221192 | tf_op jit(solution)/shard_map/ppermute | solution.py:427
  37.7 7.1 %collective-permute-start.36 = (bf16[96,384]{1,0:T(8,128)(2,1)S(1)}, bf16[96,384]{1,0:T(8,128)(2,1)S(1)}, u32[]{:S(2)}, u32[]{:S(2)}) collective-permute-start(bf16[96,384]{1,0:T(8,128)(2,1)S(1)} %get-tuple-element.120), channel_id=1, source_target_pairs={{0,16},{1,17},{2,18},{3,19},{4,20},{5,21},{6,22},{7,23},{8,24},{9,... | collective-permute-start | bytes 221192 | tf_op jit(solution)/shard_map/ppermute | solution.py:427
  39.7 6.3 %collective-permute-start.37 = (bf16[96,384]{1,0:T(8,128)(2,1)S(1)}, bf16[96,384]{1,0:T(8,128)(2,1)S(1)}, u32[]{:S(2)}, u32[]{:S(2)}) collective-permute-start(bf16[96,384]{1,0:T(8,128)(2,1)S(1)} %get-tuple-element.121), channel_id=1, source_target_pairs={{0,24},{1,25},{2,26},{3,27},{4,28},{5,29},{6,30},{7,31},{8,16},{9,... | collective-permute-start | bytes 221192 | tf_op jit(solution)/shard_map/ppermute | solution.py:427
where the time goes:
time: 47 us; the launch traced here: 46.8 us
  starting transfers between devices  17 us (36%)
  waiting for transfers between devices  14.9 us (32%)
  Pallas kernels  11.9 us (25%)
  local copies, waits for them, and re-layouts  1.39 us (3%)
  between operations  0.87 us (2%)
  other arithmetic  0.7 us (1%)
    ppermute x3, waiting for transfers between devices, reduce_near(): lax.ppermute(send, both, route(2 * (m + 1), 0))  5.48 us
    ppermute x3, starting transfers between devices, reduce_near(): lax.ppermute(send, both, route(2 * (m + 1), 0))  4.45 us
    ppermute x1, starting transfers between devices, fetch(): far = lax.ppermute(block, both, route(2))  3.4 us
    pallas_call x1, Pallas kernels, project(): pl.pallas_call(functools.partial(last_pair_kernel, grid_x, scale), out_sh...  2.6 us
    ppermute x1, starting transfers between devices, per_device(): emp_x = lax.ppermute(mine, 'row', [(i, i ^ 2) for i in range(rcount)])  2.55 us
    ppermute x1, waiting for transfers between devices, reduce_near(): from_y = lax.ppermute(to_y, both, route(1, 0))  2.5 us
    ppermute x1, waiting for transfers between devices, fetch(): far = lax.ppermute(block, both, route(2))  2.43 us
    ppermute x1, waiting for transfers between devices, reduce_near(): from_x = lax.ppermute(to_x, both, route(0, 2))  2.26 us
  transfers between devices with their start and end apart: 14, of which 8 were waited for; matrix products, arithmetic and copies ran while one was open for 4% of the time, Pallas kernels for 10%

commit v1 on v0

v1 whole, which is shorter than its diff:
```python
import functools
import math

import jax
import jax.numpy as jnp
import numpy as np
from jax import lax
from jax.experimental import pallas as pl
from jax.experimental.pallas import tpu as pltpu
from jax.sharding import PartitionSpec as P


GY = 16
GZ = 32
REACH = 4
SHIFTS = 4
LANES = 128

SIDE = 2 * REACH + 1
FACTORS = SIDE
HALF = LANES // 2


def plane_table():
    u = np.arange(HALF)
    h1 = (u + REACH) // SIDE
    h2 = u - SIDE * h1
    y, z = np.divmod(np.arange(GY * GZ), GZ)
    turns = (h1[None, :] * y[:, None] * GZ + h2[None, :] * z[:, None] * GY) % (GY * GZ)
    angle = 2.0 * np.pi * turns / (GY * GZ)
    used = (u <= (SIDE * SIDE) // 2)[None, :]
    whole = np.concatenate([np.cos(angle) * used, np.sin(angle) * used], axis=1).astype(np.float32)
    high = whole.astype(jnp.bfloat16)
    low = (whole - high.astype(np.float32)).astype(jnp.bfloat16)
    return np.concatenate([high, low], axis=1)


def column_index(waves):
    g0, flat = waves[:, 0], waves[:, 1] * SIDE + waves[:, 2]
    u = jnp.abs(flat)
    turn = jnp.where(flat < 0, -1, 1)
    side = jnp.sign(g0)
    cos_row = jnp.abs(g0) * LANES + u
    sin_row = jnp.where(g0 == 0, 0, REACH + jnp.abs(g0)) * LANES + u
    half = waves.shape[0] // 2

    def order(cosine, sine):
        return jnp.concatenate([cosine[:half], sine[:half], cosine[half:], sine[half:]])

    return jnp.stack(
        [
            order(cos_row, sin_row),
            order(sin_row + HALF, cos_row + HALF),
            order(jnp.ones_like(g0), side),
            order(-turn * side, turn),
        ]
    )


def vmem(count):
    return [pl.BlockSpec(memory_space=pltpu.VMEM)] * count


SMEM = pl.BlockSpec(memory_space=pltpu.SMEM)


def room(mebibytes):
    return pltpu.CompilerParams(vmem_limit_bytes=mebibytes << 20)


def prepare_kernel(stride, choices, table, energy, empty, occupied, choice, mine, theirs, sent, partner, level, sems):
    half = mine.shape[0]
    points = mine.shape[1]
    core = lax.axis_index("row") % 2
    parts = (core, 1 - core)
    copies = [
        pltpu.make_async_copy(empty.at[0, pl.ds(pl.multiple_of(part * half, half), half)], to, sems.at[i])
        for i, (part, to) in enumerate(zip(parts, (mine, theirs)))
    ]
    copies.append(pltpu.make_async_copy(occupied.at[0], sent.at[:, pl.ds(0, points)], sems.at[2]))
    small = [pltpu.make_async_copy(table, partner, sems.at[3]), pltpu.make_async_copy(energy, level, sems.at[4])]
    for copy in small + copies:
        copy.start()
    for copy in small:
        copy.wait()
    steps = [jnp.clip(partner[moment, 0] // stride, 1, choices) - 1 for moment in range(2)]
    choice[0, 0] = steps[0] * choices + steps[1]
    states = sent.shape[0]
    square = (states, states)
    here = lax.broadcasted_iota(jnp.int32, square, 0) == lax.broadcasted_iota(jnp.int32, square, 1)
    spread = jnp.where(here, jnp.broadcast_to(level[...].astype(jnp.float32), square), 0.0)
    column = jnp.sum(spread, axis=1, keepdims=True)
    sent[:, points:] = jnp.broadcast_to(column, (states, LANES)).astype(jnp.bfloat16)
    for copy in copies:
        copy.wait()


def prepare(partner, occ_energy, empty, occupied, stride, choices):
    _, bands, points = empty.shape
    states = occupied.shape[1]
    half = jax.ShapeDtypeStruct((bands // 2, points), jnp.bfloat16)
    return pl.pallas_call(
        functools.partial(prepare_kernel, stride, choices),
        out_shape=[
            jax.ShapeDtypeStruct((1, 1), jnp.int32),
            half,
            half,
            jax.ShapeDtypeStruct((states, points + LANES), jnp.bfloat16),
        ],
        in_specs=[pl.BlockSpec(memory_space=pltpu.HBM)] * 4,
        out_specs=[SMEM] + vmem(3),
        scratch_shapes=[
            pltpu.SMEM(partner.shape, partner.dtype),
            pltpu.VMEM(occ_energy.shape, occ_energy.dtype),
            pltpu.SemaphoreType.DMA((5,)),
        ],
        compiler_params=room(4),
        name="prepare",
    )(*[pltpu.with_memory_space_constraint(value, pltpu.HBM) for value in (partner, occ_energy, empty, occupied)])


def settle_kernel(count, *refs):
    for source, to in zip(refs[:count], refs[count:]):
        to[...] = source[...]


def settle(*blocks):
    return pl.pallas_call(
        functools.partial(settle_kernel, len(blocks)),
        out_shape=[pltpu.VMEM(block.shape, block.dtype) for block in blocks],
        in_specs=vmem(len(blocks)),
        out_specs=vmem(len(blocks)),
        compiler_params=room(2),
        name="settle",
    )(*blocks)


def whereabouts():
    r, k = lax.axis_index("row"), lax.axis_index("ka")
    return r % 2, r // 2, k % 2, k // 2


def transform(emp, occ, plane, wide, density, part, after=None):
    bands, points = emp.shape
    states = occ.shape[0]
    sheet = plane.shape[0]
    count = points // sheet
    tile = 16
    if occ.dtype != jnp.float32:
        wide[...] = occ[:, :points].astype(jnp.float32)
        occ = wide

    def fill(v):
        for step in range(count):
            at = slice(step * sheet, (step + 1) * sheet)
            row = jnp.broadcast_to(occ[v : v + 1, at], (tile, sheet)).astype(jnp.bfloat16)
            for top in range(0, bands, tile):
                density[v % 2, step * bands + top : step * bands + top + tile, :] = row * emp[top : top + tile, at]

    fill(0)
    for v in range(states):
        if v + 1 < states:
            fill(v + 1)
        made = jnp.dot(density[v % 2], plane[...], preferred_element_type=jnp.float32)
        made = made[:, :LANES] + made[:, LANES:]
        for step in range(count):
            part[step, v * bands : (v + 1) * bands, :] = made[step * bands : (step + 1) * bands]
        if after is not None and v > 0:
            after(v - 1)
    if after is not None:
        after(states - 1)


def fold_pair(pair, grid_x, near, far, bands, store):
    count = near.shape[0]
    core, x, _, _ = whereabouts()
    lower = core if pair == 0 else 1 - core
    sign = jnp.where(x == 0, jnp.float32(1), jnp.float32(-1))
    middle = (count - 1) / 2
    turn = {}
    for g in range(1, REACH + 1):
        angles = [2.0 * math.pi * g * (row * count + middle) / grid_x for row in range(2)]
        scale = sign if g % 2 else jnp.float32(1)
        turn[g] = [
            jnp.where(lower == 0, jnp.float32(part(angles[0])), jnp.float32(part(angles[1]))) * scale
            for part in (math.cos, math.sin)
        ]
    tall = 8

    def weighted(values, weights):
        total = values[0] * weights[0]
        for value, weight in zip(values[1:], weights[1:]):
            total = total + value * weight
        return total

    def after(v):
        for top in range(v * bands, (v + 1) * bands, tall):
            rows = slice(top, top + tall)
            ones = [near[step, rows, :] for step in range(count)]
            twos = [far[step, rows, :] for step in range(count)]
            for odd in (0, 1):
                both = [one - two if odd else one + two for one, two in zip(ones, twos)]
                half = count // 2
                evens = [both[half + i] + both[half - 1 - i] for i in range(half)]
                odds = [both[half + i] - both[half - 1 - i] for i in range(half)]
                if not odd:
                    store(0, rows, functools.reduce(lambda p, q: p + q, evens))
                for g in range(2 - odd, REACH + 1, 2):
                    angles = [2.0 * math.pi * g * (i + 0.5) / grid_x for i in range(half)]
                    even = weighted(evens, [math.cos(t) for t in angles])
                    rest = weighted(odds, [math.sin(t) for t in angles])
                    c, s = turn[g]
                    store(g, rows, even * c - rest * s)
                    store(REACH + g, rows, even * s + rest * c)

    return after


def first_kernel(emp, occ, plane, part, wide, density):
    transform(emp, occ, plane, wide, density, part)


def own_kernel(emp, occ, plane, energy, part, w_own, w_other, wide, density):
    bands, points = emp.shape
    states = occ.shape[0]
    core = whereabouts()[0]
    shape = (bands, energy.shape[1])
    down = lax.broadcasted_iota(jnp.int32, shape, 0)
    along = lax.broadcasted_iota(jnp.int32, shape, 1)
    levels = jnp.broadcast_to(energy[...].astype(jnp.float32), shape)
    for part_of, weight in ((core, w_own), (1 - core, w_other)):
        column = jnp.sum(jnp.where(along == down + part_of * bands, levels, 0.0), axis=1, keepdims=True)
        column = jnp.broadcast_to(column, (bands, LANES))
        for v in range(states):
            level = occ[v : v + 1, points : points + LANES].astype(jnp.float32)
            weight[v * bands : (v + 1) * bands, :] = 1.0 / (column - level)
    transform(emp, occ, plane, wide, density, part)


def matrix_kernel(index, matrix):
    share = 2 * LANES // 4
    shape = (share, matrix.shape[1])
    signs = index[2:4, :].astype(jnp.float32)

    def body(at, carry):
        start = pl.multiple_of(at * share, share)
        rows = lax.broadcasted_iota(jnp.int32, shape, 0) + start
        two = jnp.where(rows == index[1:2, :], jnp.broadcast_to(signs[1:2], shape), 0.0)
        one = jnp.where(rows == index[0:1, :], jnp.broadcast_to(signs[0:1], shape), two)
        matrix[pl.ds(start, share), :] = one.astype(jnp.bfloat16)
        return carry

    lax.fori_loop(0, matrix.shape[0] // share, body, 0)


def make_matrix(index):
    return pl.pallas_call(
        matrix_kernel,
        out_shape=pltpu.VMEM((FACTORS * LANES, index.shape[1]), jnp.bfloat16),
        in_specs=vmem(1),
        out_specs=vmem(1)[0],
        compiler_params=room(4),
        name="matrix",
    )(index)


def fold_pair(pair, grid_x, near, far, bands, store):
    count = near.shape[0]
    core, x, _, _ = whereabouts()
    lower = core if pair == 0 else 1 - core
    sign = jnp.where(x == 0, jnp.float32(1), jnp.float32(-1))
    middle = (count - 1) / 2
    turn = {}
    for g in range(1, REACH + 1):
        angles = [2.0 * math.pi * g * (row * count + middle) / grid_x for row in range(2)]
        scale = sign if g % 2 else jnp.float32(1)
        turn[g] = [
            jnp.where(lower == 0, jnp.float32(part(angles[0])), jnp.float32(part(angles[1]))) * scale
            for part in (math.cos, math.sin)
        ]
    tall = 8

    def weighted(values, weights):
        total = values[0] * weights[0]
        for value, weight in zip(values[1:], weights[1:]):
            total = total + value * weight
        return total

    def after(v):
        for top in range(v * bands, (v + 1) * bands, tall):
            rows = slice(top, top + tall)
            ones = [near[step, rows, :] for step in range(count)]
            twos = [far[step, rows, :] for step in range(count)]
            for odd in (0, 1):
                both = [one - two if odd else one + two for one, two in zip(ones, twos)]
                half = count // 2
                evens = [both[half + i] + both[half - 1 - i] for i in range(half)]
                odds = [both[half + i] - both[half - 1 - i] for i in range(half)]
                if not odd:
                    store(0, rows, functools.reduce(lambda p, q: p + q, evens))
                for g in range(2 - odd, REACH + 1, 2):
                    angles = [2.0 * math.pi * g * (i + 0.5) / grid_x for i in range(half)]
                    even = weighted(evens, [math.cos(t) for t in angles])
                    rest = weighted(odds, [math.sin(t) for t in angles])
                    c, s = turn[g]
                    store(g, rows, even * c - rest * s)
                    store(REACH + g, rows, even * s + rest * c)

    return after


def first_kernel(emp, occ, plane, part, wide, density):
    transform(emp, occ, plane, wide, density, part)


def middle_pair_kernel(grid_x, emp, occ, plane, near, total, wide, density, part):
    def store(j, rows, value):
        total[j, rows, :] = value

    transform(emp, occ, plane, wide, density, part, fold_pair(0, grid_x, near, part, emp.shape[0], store))


def last_pair_kernel(
    grid_x, scale, emp, occ, plane, near, before, matrix, left, wide, density, part, total, narrow
):
    def store(j, rows, value):
        total[j, rows, :] = before[j, rows, :] + value

    transform(emp, occ, plane, wide, density, part, fold_pair(1, grid_x, near, part, emp.shape[0], store))
    for j in range(FACTORS):
        narrow[:, j * LANES : (j + 1) * LANES] = total[j].astype(jnp.bfloat16)
    proj = jnp.dot(narrow[...], matrix[...], preferred_element_type=jnp.float32)
    left[...] = (proj * scale).astype(jnp.bfloat16)


def scratch_of(emp, states):
    bands, points = emp.shape
    sheet = GY * GZ
    return [
        pltpu.VMEM((states, points), jnp.float32),
        pltpu.VMEM((2, points // sheet * bands, sheet), jnp.bfloat16),
    ]


def project(matrix, blocks, energy, grid_x, scale):
    (own, core, x, far) = blocks
    bands, points = core[0].shape
    states = core[1].shape[0]
    pairs = bands * states
    count = points // (GY * GZ)
    columns = matrix.shape[1]
    plane = jnp.asarray(plane_table())
    part_shape = (count, pairs, LANES)
    total_shape = (FACTORS, pairs, LANES)
    scratch = scratch_of(core[0], states)
    part = pltpu.VMEM(part_shape, jnp.float32)

    def first(kernel, outs, operands):
        return pl.pallas_call(
            kernel,
            out_shape=[jax.ShapeDtypeStruct(shape, jnp.float32) for shape in outs],
            in_specs=vmem(len(operands)),
            out_specs=vmem(len(outs)),
            scratch_shapes=scratch,
            compiler_params=room(6),
        )(*operands)

    weight_shape = (pairs, LANES)
    part_own, w_own, w_other = first(own_kernel, [part_shape] + [weight_shape] * 2, (*own, plane, energy))
    (part_core,) = first(first_kernel, [part_shape], (*core, plane))
    total = pl.pallas_call(
        functools.partial(middle_pair_kernel, grid_x),
        out_shape=jax.ShapeDtypeStruct(total_shape, jnp.float32),
        in_specs=vmem(4),
        out_specs=vmem(1)[0],
        scratch_shapes=scratch + [part],
        compiler_params=room(8),
        name="pair",
    )(*x, plane, part_own)
    left = pl.pallas_call(
        functools.partial(last_pair_kernel, grid_x, scale),
        out_shape=jax.ShapeDtypeStruct((pairs, columns), jnp.bfloat16),
        in_specs=vmem(6),
        out_specs=vmem(1)[0],
        scratch_shapes=scratch
        + [part, pltpu.VMEM(total_shape, jnp.float32), pltpu.VMEM((pairs, FACTORS * LANES), jnp.bfloat16)],
        compiler_params=room(14),
        name="last",
    )(*far, plane, part_core, total, matrix)
    return left, w_own, w_other


def gram_of(core, values, weights):
    width = values.shape[1] // 2
    at = pl.multiple_of(core * width, LANES)
    right = [
        (values[:, pl.ds(at + tile * LANES, LANES)].astype(jnp.float32) * weights[...]).astype(jnp.bfloat16)
        for tile in range(width // LANES)
    ]
    return lax.dot_general(
        values[...], jnp.concatenate(right, axis=1), (((0,), (0,)), ((), ())), preferred_element_type=jnp.float32
    )


def gram_own_kernel(own, w_own, gram):
    gram[...] = gram_of(whereabouts()[0], own, w_own)


def roll_half(value):
    return pltpu.roll(value, value.shape[1] // 2, 1)


def gram_kernel(first, other, w_other, keep, to_y, to_z, to_yz, gram):
    core, _, y, z = whereabouts()
    zl = z % 2
    gram[...] = first[...] + gram_of(core, other, w_other)
    rows = gram.shape[0] // 8
    for out, to_y_of, to_zl in ((keep, y, zl), (to_y, 1 - y, zl), (to_z, y, 1 - zl), (to_yz, 1 - y, 1 - zl)):
        for zh in range(2):
            start = ((2 * to_zl + zh) * 2 + to_y_of) * rows
            out[zh * rows : (zh + 1) * rows, :] = gram[pl.ds(pl.multiple_of(start, 8), rows), :].astype(out.dtype)


def middle_kernel(keep, from_y, from_z, from_yz, stay, to_x, to_z, to_xz, total):
    _, x, _, z = whereabouts()
    zh = z // 2
    rows = keep.shape[0] // 2
    total[...] = (keep[...] + from_y[...].astype(jnp.float32)) + (
        from_z[...].astype(jnp.float32) + from_yz[...].astype(jnp.float32)
    )
    low = lax.broadcasted_iota(jnp.int32, (rows // 2, keep.shape[1]), 1) < keep.shape[1] // 2
    for to_zh, near, far in ((zh, stay, to_x), (1 - zh, to_z, to_xz)):
        top = total[pl.ds(pl.multiple_of(to_zh * rows, 8), rows // 2), :]
        bottom = total[pl.ds(pl.multiple_of(to_zh * rows + rows // 2, 8), rows // 2), :]
        zero = jnp.where(low, top, roll_half(bottom))
        one = jnp.where(low, roll_half(top), bottom)
        near[...] = jnp.where(x == 0, zero, one).astype(near.dtype)
        far[...] = jnp.where(x == 0, one, zero).astype(far.dtype)


def final_kernel(stay, from_x, from_z, from_xz, out):
    x = whereabouts()[1]
    same = stay[...] + from_z[...].astype(jnp.float32)
    cross = from_x[...].astype(jnp.float32) + from_xz[...].astype(jnp.float32)
    rows, width = same.shape[0], same.shape[1] // 2
    for moment in range(2):
        value = jnp.where(x == moment, same, cross)
        out[moment, :rows, :] = value[:, :width]
        out[moment, rows:, :] = roll_half(value)[:, :width]


def reduce_near(own, other, w_own, w_other):
    wide = own.shape[1]
    kcount, rcount = lax.axis_size("ka"), lax.axis_size("row")
    bf16, f32 = jnp.bfloat16, jnp.float32
    first = pl.pallas_call(
        gram_own_kernel,
        out_shape=jax.ShapeDtypeStruct((wide, wide // 2), f32),
        in_specs=vmem(2),
        out_specs=vmem(1)[0],
        compiler_params=room(8),
        name="gram_own",
    )(own, w_own)
    quarter = (wide // 4, wide // 2)
    keep, *sends = pl.pallas_call(
        gram_kernel,
        out_shape=[jax.ShapeDtypeStruct(quarter, d) for d in (f32, bf16, bf16, bf16)],
        in_specs=vmem(3),
        out_specs=vmem(4),
        scratch_shapes=[pltpu.VMEM((wide, wide // 2), f32)],
        compiler_params=room(10),
        name="gram",
    )(first, other, w_other)

    def exchange(values, ways):
        came = []
        for value, (dk, dr) in zip(values, ways):
            pairs = [(k * rcount + r, (k ^ dk) * rcount + (r ^ dr)) for k in range(kcount) for r in range(rcount)]
            came.append(lax.ppermute(value, ("ka", "row"), pairs))
        return came

    came = exchange(sends, ((1, 0), (2, 0), (3, 0)))
    piece = (quarter[0] // 4, quarter[1])
    stay, *sends = pl.pallas_call(
        middle_kernel,
        out_shape=[jax.ShapeDtypeStruct(piece, d) for d in (f32, bf16, bf16, bf16)],
        in_specs=vmem(4),
        out_specs=vmem(4),
        scratch_shapes=[pltpu.VMEM(quarter, f32)],
        compiler_params=room(6),
        name="middle",
    )(keep, *came)
    came = exchange(sends, ((0, 2), (4, 0), (4, 2)))
    return pl.pallas_call(
        final_kernel,
        out_shape=jax.ShapeDtypeStruct((2, piece[0] * 2, piece[1] // 2), f32),
        in_specs=vmem(4),
        out_specs=vmem(1)[0],
        compiler_params=room(4),
        name="final",
    )(stay, *came)


def reduce_far(own, other, w_own, w_other):
    kcount = lax.axis_size("ka")
    core, x, _, _ = whereabouts()
    wide = own.shape[1]
    width = wide // 4
    left = jnp.concatenate([own, other], axis=0)
    weight = jnp.concatenate([w_own[:, :1], w_other[:, :1]], axis=0)
    right = lax.dynamic_slice_in_dim(left, core * 2 * width, 2 * width, 1)
    right = (right.astype(jnp.float32) * weight).astype(jnp.bfloat16)
    gram = lax.dot_general(left, right, (((0,), (0,)), ((), ())), preferred_element_type=jnp.float32)
    gram = gram.reshape(2, 2, width, 2, width).swapaxes(0, 1).reshape(kcount, wide // kcount, 2, width)
    parts = lax.all_to_all(gram.astype(jnp.bfloat16), "ka", 0, 0, tiled=True)
    total = jnp.sum(parts.astype(jnp.float32), axis=0)
    mine = lax.dynamic_index_in_dim(total, x, 1, keepdims=False)
    send = lax.dynamic_index_in_dim(total, 1 - x, 1, keepdims=False)
    came = lax.ppermute(send, "row", [(r, r ^ 2) for r in range(lax.axis_size("row"))])
    first = x == 0
    return jnp.stack([jnp.where(first, mine, came), jnp.where(first, came, mine)])


def per_device(occupied, empty, occ_energy, emp_energy, partner, gvecs):
    kcount, rcount = lax.axis_size("ka"), lax.axis_size("row")
    assert rcount == 4 and partner.shape[0] == 2
    r = lax.axis_index("row")
    x = r // 2
    points = occupied.shape[2]
    grid_x = points * rcount // (GY * GZ)
    stride = kcount // min(SHIFTS, kcount)
    choices = min(SHIFTS, kcount) - 1
    choice, mine, theirs, sent = prepare(partner, occ_energy, empty, occupied, stride, choices)
    emp_x = lax.ppermute(mine, "row", [(i, i ^ 2) for i in range(rcount)])
    emp_xc = lax.ppermute(theirs, "row", [(i, i ^ 3) for i in range(rcount)])
    emp_c = lax.ppermute(theirs, "row", [(i, i ^ 1) for i in range(rcount)])

    swap = [(i, i ^ 1) for i in range(rcount)]

    def fetch(shift, operands):
        block, waves = operands

        def route(dx):
            pairs = []
            for i in range(kcount):
                for j in range(rcount):
                    to = j ^ dx
                    pairs.append((i * rcount + j, (i + shift[to // 2] * stride) % kcount * rcount + to))
            return pairs

        both = ("ka", "row")
        far = lax.ppermute(block, both, route(2))
        near = lax.ppermute(block, both, route(0))
        near_c = lax.ppermute(near, "row", swap)
        matrix = make_matrix(column_index(lax.dynamic_index_in_dim(waves, x, 0, keepdims=False)))
        return *settle(near, near_c, far), matrix

    branches = [functools.partial(fetch, (one + 1, two + 1)) for one in range(choices) for two in range(choices)]
    occ_own, occ_c, occ_x, matrix = lax.switch(choice[0, 0], branches, (sent, gvecs))
    occ_xc = lax.ppermute(occ_x, "row", swap)

    blocks = ((mine, occ_own), (emp_c, occ_c), (emp_x, occ_x), (emp_xc, occ_xc))
    left, w_own, w_other = project(matrix, blocks, emp_energy, grid_x, 1.0 / (points * rcount))
    other = lax.ppermute(left, "row", swap)
    reduce = reduce_near if kcount == 8 else reduce_far
    return reduce(left, other, w_own, w_other)


def solution(mesh):
    placed = (P("ka", None, "row"), P("ka", None, "row"), P("ka", None), P("ka", None), P(), P())

    return jax.shard_map(per_device, mesh=mesh, in_specs=placed, out_specs=P(None, "ka", "row"), check_vma=False)
```

time: 47 us -> 43.9 us (0.934)
  Pallas kernels: 11.9 us -> 8.98 us
    ppermute x1, waiting for transfers between devices: 0.01 us -> 0.95 us  [per_device(): other = lax.ppermute(left, 'row', swap)]
    pallas_call x1, Pallas kernels: 1.28 us -> 0.47 us  [reduce_near(): pl.pallas_call(gram_kernel, out_shape=[jax.ShapeDtypeStruct(quarter, d) f...]
    ppermute x1, waiting for transfers between devices: 2.43 us -> 1.63 us  [fetch(): far = lax.ppermute(block, both, route(2))]
    pallas_call x4 -> x5, Pallas kernels: 3.72 us -> 3.11 us  [the longest x2 1.42 us: first(): pl.pallas_call(kernel, out_shape=[jax.ShapeDtypeStruct(shape, jnp.float32...]
    pallas_call x1, Pallas kernels: 2.6 us -> 2.02 us  [project(): pl.pallas_call(functools.partial(last_pair_kernel, grid_x, scale), out_sh...]
    pallas_call x1, Pallas kernels: 1.75 us -> 1.17 us  [project(): pl.pallas_call(functools.partial(middle_pair_kernel, grid_x), out_shape=j...]
    ppermute x1, starting transfers between devices: 0.56 us -> 0.01 us  [per_device(): emp_c = lax.ppermute(theirs, 'row', [(i, i ^ 1) for i in range(rcount)])]
    pallas_call x1, Pallas kernels: 0.94 us -> 0.4 us  [reduce_near(): pl.pallas_call(gram_own_kernel, out_shape=jax.ShapeDtypeStruct((wide, wid...]
  transfers between devices with their start and end apart: 14 -> 14, of which waited for: 8 -> 7; matrix products, arithmetic and copies ran while one was open for 4% -> 3% of each run, Pallas kernels for 10% -> 8%
where the time goes in v1:
time: 43.9 us; the launch traced here: 43.7 us
  starting transfers between devices  17.4 us (40%)
  waiting for transfers between devices  15 us (34%)
  Pallas kernels  8.98 us (20%)
  local copies, waits for them, and re-layouts  1.04 us (2%)
  between operations  0.8 us (2%)
    ppermute x6, waiting for transfers between devices, exchange(): came.append(lax.ppermute(value, ('ka', 'row'), pairs))  12.4 us
    ppermute x6, starting transfers between devices, exchange(): came.append(lax.ppermute(value, ('ka', 'row'), pairs))  8.01 us
    ppermute x1, starting transfers between devices, fetch(): far = lax.ppermute(block, both, route(2))  3.4 us
    ppermute x1, starting transfers between devices, per_device(): emp_x = lax.ppermute(mine, 'row', [(i, i ^ 2) for i in range(rcount)])  3.03 us
    ppermute x1, starting transfers between devices, fetch(): near = lax.ppermute(block, both, route(0))  2.09 us
    pallas_call x1, Pallas kernels, project(): pl.pallas_call(functools.partial(last_pair_kernel, grid_x, scale), out_sh...  2.02 us
    pallas_call x1, Pallas kernels, prepare(): pl.pallas_call(functools.partial(prepare_kernel, stride, choices), out_sh...  1.81 us
    ppermute x1, waiting for transfers between devices, fetch(): far = lax.ppermute(block, both, route(2))  1.63 us
  transfers between devices with their start and end apart: 14, of which 7 were waited for; matrix products, arithmetic and copies ran while one was open for 3% of the time, Pallas kernels for 8%

profile of v1, /device:TPU:0, one launch (start us, length us, event | category | flops | bytes accessed | tf_op | source)
XLA Modules:
  0.0 43.7 jit_solution(8951167885428951440)
XLA Ops:
  0.0 1.8 %prepare.1 = (s32[1,1]{1,0:T(1,128)}, bf16[32,4096]{1,0:T(8,128)(2,1)S(1)}, bf16[32,4096]{1,0:T(8,128)(2,1)}, bf16[8,4224]{1,0:T(8,128)(2,1)S(1)}) custom-call(s32[2,8]{1,0:T(2,128)} %table.1, bf16[1,8]{1,0:T(2,128)(2,1)} %energy.2, bf16[1,64,4096]{2,1,0:T(8,128)(2,1)} %empty.1, bf16[1,8,4096]{2,1,0:T(8,128)(2,1)} %occupied.1), custom_call_target="tpu_custom_call" | custom-call | tf_op jit(solution)/shard_map/prepare/pallas_call | solution.py:102
  1.8 3.0 %collective-permute-start.30 = (bf16[32,4096]{1,0:T(8,128)(2,1)S(1)}, bf16[32,4096]{1,0:T(8,128)(2,1)S(1)}, u32[]{:S(2)}, u32[]{:S(2)}) collective-permute-start(bf16[32,4096]{1,0:T(8,128)(2,1)S(1)} %get-tuple-element.137.emp), channel_id=1, source_target_pairs={{0,2},{1,3},{2,0},{3,1},{4,6},{5,7},{6,4},{7,5},{8,10},{9,11},{10,... | collective-permute-start | bytes 786440 | tf_op jit(solution)/shard_map/ppermute | solution.py:534
  5.7 9.4 %conditional.1 = (bf16[8,4224]{1,0:T(8,128)(2,1)S(1)}, bf16[8,4224]{1,0:T(8,128)(2,1)S(1)}, bf16[8,4224]{1,0:T(8,128)(2,1)S(1)}, bf16[1152,768]{1,0:T(8,128)(2,1)S(1)}) conditional(s32[]{:T(128)} %bitcast.135, (bf16[8,4224]{1,0:T(8,128)(2,1)S(1)}, s32[]{:T(128)}, s32[2,384,3]{1,0,2:T(2,128)}) %tuple.41, ...), branch_computations={%region_0.1_spmd, %region_1.2_spmd, %region_2.3_spmd, %region_3.4_... | conditional | flops 26115 | bytes 954050 | solution.py:559
  5.8 2.1 %collective-permute-start.6 = (bf16[8,4224]{1,0:T(8,128)(2,1)S(1)}, bf16[8,4224]{1,0:T(8,128)(2,1)S(1)}, u32[]{:S(2)}, u32[]{:S(2)}) collective-permute-start(bf16[8,4224]{1,0:T(8,128)(2,1)S(1)} %get-tuple-element.71), channel_id=1, source_target_pairs={{0,8},{1,9},{2,26},{3,27},{4,12},{5,13},{6,30},{7,31},{8,16},{9,17... | collective-permute-start | bytes 202760 | tf_op jit(solution)/shard_map/cond/branch_2_fun/ppermute | solution.py:553
  7.8 3.4 %collective-permute-start.8 = (bf16[8,4224]{1,0:T(8,128)(2,1)S(1)}, bf16[8,4224]{1,0:T(8,128)(2,1)S(1)}, u32[]{:S(2)}, u32[]{:S(2)}) collective-permute-start(bf16[8,4224]{1,0:T(8,128)(2,1)S(1)} %get-tuple-element.71), channel_id=1, source_target_pairs={{0,26},{1,27},{2,8},{3,9},{4,30},{5,31},{6,12},{7,13},{8,2},{9,3},... | collective-permute-start | bytes 202760 | tf_op jit(solution)/shard_map/cond/branch_2_fun/ppermute | solution.py:552
  11.2 0.7 %copy.10 = s32[2,384,3]{1,2,0:T(4,128)S(1)} copy(s32[2,384,3]{1,0,2:T(2,128)} %get-tuple-element.159) | data formatting | bytes 18432 | tf_op jit(solution)/shard_map
  12.7 0.7 %matrix.11 = bf16[1152,768]{1,0:T(8,128)(2,1)S(1)} custom-call(s32[4,768]{1,0:T(4,128)S(1)} %pad_add_fusion.10.index), custom_call_target="tpu_custom_call" | custom-call | tf_op jit(solution)/shard_map/cond/branch_2_fun/matrix/pallas_call | solution.py:257
  13.4 1.6 %collective-permute-done.8.refs_2_ = bf16[8,4224]{1,0:T(8,128)(2,1)S(1)} collective-permute-done((bf16[8,4224]{1,0:T(8,128)(2,1)S(1)}, bf16[8,4224]{1,0:T(8,128)(2,1)S(1)}, u32[]{:S(2)}, u32[]{:S(2)}) %collective-permute-start.8) | collective-permute-done | bytes 67616 | tf_op jit(solution)/shard_map/cond/branch_2_fun/ppermute | solution.py:552
  15.2 0.7 %shard_map.74 = (f32[8,256,128]{2,1,0:T(8,128)S(1)}, f32[256,128]{1,0:T(8,128)S(1)}, f32[256,128]{1,0:T(8,128)S(1)}) custom-call(bf16[32,4096]{1,0:T(8,128)(2,1)S(1)} %get-tuple-element.137.emp, bf16[8,4224]{1,0:T(8,128)(2,1)S(1)} %get-tuple-element.138.occ, bf16[512,256]{1,0:T(8,128)(2,1)S(1)} %copy-done, bf16[1,64]{1,0:T(2,128)(2,1)S(1)} %copy-done.1), custom_call_target="tpu_custom_call" | custom-call | tf_op jit(solution)/shard_map/pallas_call | solution.py:359
  15.9 1.2 %pair.1.before = f32[9,256,128]{2,1,0:T(8,128)S(1)} custom-call(bf16[32,4096]{1,0:T(8,128)(2,1)S(1)} %collective-permute-done.30.emp, bf16[8,4224]{1,0:T(8,128)(2,1)S(1)} %get-tuple-element.135.occ, bf16[512,256]{1,0:T(8,128)(2,1)S(1)} %copy-done, f32[8,256,128]{2,1,0:T(8,128)S(1)} %get-tuple-element.139.near), custom_call_target="tpu_custom_call" | custom-call | tf_op jit(solution)/shard_map/pair/pallas_call | solution.py:371
  17.1 0.7 %shard_map.73.near = f32[8,256,128]{2,1,0:T(8,128)S(1)} custom-call(bf16[32,4096]{1,0:T(8,128)(2,1)S(1)} %collective-permute-done.29.emp, bf16[8,4224]{1,0:T(8,128)(2,1)S(1)} %get-tuple-element.136.occ, bf16[512,256]{1,0:T(8,128)(2,1)S(1)} %copy-done), custom_call_target="tpu_custom_call" | custom-call | tf_op jit(solution)/shard_map/pallas_call | solution.py:359
  17.8 2.0 %last.1.own = bf16[256,768]{1,0:T(8,128)(2,1)S(1)} custom-call(bf16[32,4096]{1,0:T(8,128)(2,1)S(1)} %collective-permute-done.27.emp, bf16[8,4224]{1,0:T(8,128)(2,1)S(1)} %collective-permute-done.28.occ, bf16[512,256]{1,0:T(8,128)(2,1)S(1)} %copy-done, f32[8,256,128]{2,1,0:T(8,128)S(1)} %shard_map.73.near, f32[9,256,128]{2,1,0:T(8,128)S(1)} %pair.1.before, ...), custom_call_target="tpu_custom_call" | custom-call | tf_op jit(solution)/shard_map/last/pallas_call | solution.py:380
  19.9 0.5 %collective-permute-start.31 = (bf16[256,768]{1,0:T(8,128)(2,1)S(1)}, bf16[256,768]{1,0:T(8,128)(2,1)S(1)}, u32[]{:S(2)}, u32[]{:S(2)}) collective-permute-start(bf16[256,768]{1,0:T(8,128)(2,1)S(1)} %last.1.own), channel_id=1, source_target_pairs={{0,1},{1,0},{2,3},{3,2},{4,5},{5,4},{6,7},{7,6},{8,9},{9,8},{10,11... | collective-permute-start | bytes 1179656 | tf_op jit(solution)/shard_map/ppermute | solution.py:564
  20.8 0.9 %collective-permute-done.31.other = bf16[256,768]{1,0:T(8,128)(2,1)S(1)} collective-permute-done((bf16[256,768]{1,0:T(8,128)(2,1)S(1)}, bf16[256,768]{1,0:T(8,128)(2,1)S(1)}, u32[]{:S(2)}, u32[]{:S(2)}) %collective-permute-start.31) | collective-permute-done | bytes 393248 | tf_op jit(solution)/shard_map/ppermute | solution.py:564
  22.2 1.6 %collective-permute-start.32 = (bf16[192,384]{1,0:T(8,128)(2,1)S(1)}, bf16[192,384]{1,0:T(8,128)(2,1)S(1)}, u32[]{:S(2)}, u32[]{:S(2)}) collective-permute-start(bf16[192,384]{1,0:T(8,128)(2,1)S(1)} %get-tuple-element.144), channel_id=1, source_target_pairs={{0,4},{1,5},{2,6},{3,7},{4,0},{5,1},{6,2},{7,3},{8,12},{9,13},{10,... | collective-permute-start | bytes 442376 | tf_op jit(solution)/shard_map/ppermute | solution.py:479
  23.8 1.5 %collective-permute-start.33 = (bf16[192,384]{1,0:T(8,128)(2,1)S(1)}, bf16[192,384]{1,0:T(8,128)(2,1)S(1)}, u32[]{:S(2)}, u32[]{:S(2)}) collective-permute-start(bf16[192,384]{1,0:T(8,128)(2,1)S(1)} %get-tuple-element.145), channel_id=1, source_target_pairs={{0,8},{1,9},{2,10},{3,11},{4,12},{5,13},{6,14},{7,15},{8,0},{9,1},... | collective-permute-start | bytes 442376 | tf_op jit(solution)/shard_map/ppermute | solution.py:479
  25.8 2.6 %collective-permute-done.32.from_y = bf16[192,384]{1,0:T(8,128)(2,1)S(1)} collective-permute-done((bf16[192,384]{1,0:T(8,128)(2,1)S(1)}, bf16[192,384]{1,0:T(8,128)(2,1)S(1)}, u32[]{:S(2)}, u32[]{:S(2)}) %collective-permute-start.32) | collective-permute-done | bytes 147488 | tf_op jit(solution)/shard_map/ppermute | solution.py:479
  28.4 2.1 %collective-permute-done.33.from_z = bf16[192,384]{1,0:T(8,128)(2,1)S(1)} collective-permute-done((bf16[192,384]{1,0:T(8,128)(2,1)S(1)}, bf16[192,384]{1,0:T(8,128)(2,1)S(1)}, u32[]{:S(2)}, u32[]{:S(2)}) %collective-permute-start.33) | collective-permute-done | bytes 147488 | tf_op jit(solution)/shard_map/ppermute | solution.py:479
  30.6 2.2 %collective-permute-done.34.from_yz = bf16[192,384]{1,0:T(8,128)(2,1)S(1)} collective-permute-done((bf16[192,384]{1,0:T(8,128)(2,1)S(1)}, bf16[192,384]{1,0:T(8,128)(2,1)S(1)}, u32[]{:S(2)}, u32[]{:S(2)}) %collective-permute-start.34) | collective-permute-done | bytes 147488 | tf_op jit(solution)/shard_map/ppermute | solution.py:479
  33.0 1.5 %collective-permute-start.35 = (bf16[48,384]{1,0:T(8,128)(2,1)S(1)}, bf16[48,384]{1,0:T(8,128)(2,1)S(1)}, u32[]{:S(2)}, u32[]{:S(2)}) collective-permute-start(bf16[48,384]{1,0:T(8,128)(2,1)S(1)} %get-tuple-element.148), channel_id=1, source_target_pairs={{0,2},{1,3},{2,0},{3,1},{4,6},{5,7},{6,4},{7,5},{8,10},{9,11},{10,... | collective-permute-start | bytes 110600 | tf_op jit(solution)/shard_map/ppermute | solution.py:479
  34.6 2.6 %collective-permute-start.36 = (bf16[48,384]{1,0:T(8,128)(2,1)S(1)}, bf16[48,384]{1,0:T(8,128)(2,1)S(1)}, u32[]{:S(2)}, u32[]{:S(2)}) collective-permute-start(bf16[48,384]{1,0:T(8,128)(2,1)S(1)} %get-tuple-element.149), channel_id=1, source_target_pairs={{0,16},{1,17},{2,18},{3,19},{4,20},{5,21},{6,22},{7,23},{8,24},{9,... | collective-permute-start | bytes 110600 | tf_op jit(solution)/shard_map/ppermute | solution.py:479
  37.5 2.1 %collective-permute-done.36.from_z = bf16[48,384]{1,0:T(8,128)(2,1)S(1)} collective-permute-done((bf16[48,384]{1,0:T(8,128)(2,1)S(1)}, bf16[48,384]{1,0:T(8,128)(2,1)S(1)}, u32[]{:S(2)}, u32[]{:S(2)}) %collective-permute-start.36) | collective-permute-done | bytes 36896 | tf_op jit(solution)/shard_map/ppermute | solution.py:479
  39.6 3.3 %collective-permute-done.37.from_xz = bf16[48,384]{1,0:T(8,128)(2,1)S(1)} collective-permute-done((bf16[48,384]{1,0:T(8,128)(2,1)S(1)}, bf16[48,384]{1,0:T(8,128)(2,1)S(1)}, u32[]{:S(2)}, u32[]{:S(2)}) %collective-permute-start.37) | collective-permute-done | bytes 36896 | tf_op jit(solution)/shard_map/ppermute | solution.py:479
  42.9 0.8 %final.1 = f32[2,96,192]{2,1,0:T(8,128)} custom-call(f32[48,384]{1,0:T(8,128)S(1)} %get-tuple-element.147.stay, bf16[48,384]{1,0:T(8,128)(2,1)S(1)} %collective-permute-done.35.from_x, bf16[48,384]{1,0:T(8,128)(2,1)S(1)} %collective-permute-done.36.from_z, bf16[48,384]{1,0:T(8,128)(2,1)S(1)} %collective-permute-done.37.from_xz), custom_call_target="tpu_custom_call" | custom-call | tf_op jit(solution)/shard_map/final/pallas_call | solution.py:494
  (38 shorter events, 2.9 us)
Async XLA Ops:
  1.8 14.1 %collective-permute-start.30 = (bf16[32,4096]{1,0:T(8,128)(2,1)S(1)}, bf16[32,4096]{1,0:T(8,128)(2,1)S(1)}, u32[]{:S(2)}, u32[]{:S(2)}) collective-permute-start(bf16[32,4096]{1,0:T(8,128)(2,1)S(1)} %get-tuple-element.137.emp), channel_id=1, source_target_pairs={{0,2},{1,3},{2,0},{3,1},{4,6},{5,7},{6,4},{7,5},{8,10},{9,11},{10,... | collective-permute-start | bytes 786440 | tf_op jit(solution)/shard_map/ppermute | solution.py:534
  4.8 12.2 %collective-permute-start.29 = (bf16[32,4096]{1,0:T(8,128)(2,1)}, bf16[32,4096]{1,0:T(8,128)(2,1)S(1)}, u32[]{:S(2)}, u32[]{:S(2)}) collective-permute-start(bf16[32,4096]{1,0:T(8,128)(2,1)} %get-tuple-element.132), channel_id=1, source_target_pairs={{0,1},{1,0},{2,3},{3,2},{4,5},{5,4},{6,7},{7,6},{8,9},{9,8},{10,11... | collective-permute-start | bytes 786440 | tf_op jit(solution)/shard_map/ppermute | solution.py:536
  4.9 13.0 %collective-permute-start.27 = (bf16[32,4096]{1,0:T(8,128)(2,1)}, bf16[32,4096]{1,0:T(8,128)(2,1)S(1)}, u32[]{:S(2)}, u32[]{:S(2)}) collective-permute-start(bf16[32,4096]{1,0:T(8,128)(2,1)} %get-tuple-element.132), channel_id=1, source_target_pairs={{0,3},{1,2},{2,1},{3,0},{4,7},{5,6},{6,5},{7,4},{8,11},{9,10},{10,... | collective-permute-start | bytes 786440 | tf_op jit(solution)/shard_map/ppermute | solution.py:535
  5.7 9.5 %copy-start = (bf16[512,256]{1,0:T(8,128)(2,1)S(1)}, bf16[512,256]{1,0:T(8,128)(2,1)}, u32[]{:S(2)}) copy-start(bf16[512,256]{1,0:T(8,128)(2,1)} %constant.199.clone.plane) | copy-start | bytes 786436
  5.7 9.5 %copy-start.1 = (bf16[1,64]{1,0:T(2,128)(2,1)S(1)}, bf16[1,64]{1,0:T(2,128)(2,1)}, u32[]{:S(2)}) copy-start(bf16[1,64]{1,0:T(2,128)(2,1)} %energy.3) | copy-start | bytes 388
  5.8 6.9 %collective-permute-start.6 = (bf16[8,4224]{1,0:T(8,128)(2,1)S(1)}, bf16[8,4224]{1,0:T(8,128)(2,1)S(1)}, u32[]{:S(2)}, u32[]{:S(2)}) collective-permute-start(bf16[8,4224]{1,0:T(8,128)(2,1)S(1)} %get-tuple-element.71), channel_id=1, source_target_pairs={{0,8},{1,9},{2,26},{3,27},{4,12},{5,13},{6,30},{7,31},{8,16},{9,17... | collective-permute-start | bytes 202760 | tf_op jit(solution)/shard_map/cond/branch_2_fun/ppermute | solution.py:553
  7.8 7.2 %collective-permute-start.8 = (bf16[8,4224]{1,0:T(8,128)(2,1)S(1)}, bf16[8,4224]{1,0:T(8,128)(2,1)S(1)}, u32[]{:S(2)}, u32[]{:S(2)}) collective-permute-start(bf16[8,4224]{1,0:T(8,128)(2,1)S(1)} %get-tuple-element.71), channel_id=1, source_target_pairs={{0,26},{1,27},{2,8},{3,9},{4,30},{5,31},{6,12},{7,13},{8,2},{9,3},... | collective-permute-start | bytes 202760 | tf_op jit(solution)/shard_map/cond/branch_2_fun/ppermute | solution.py:552
  12.6 2.4 %collective-permute-start.7 = (bf16[8,4224]{1,0:T(8,128)(2,1)S(1)}, bf16[8,4224]{1,0:T(8,128)(2,1)S(1)}, u32[]{:S(2)}, u32[]{:S(2)}) collective-permute-start(bf16[8,4224]{1,0:T(8,128)(2,1)S(1)} %collective-permute-done.6.refs_0_), channel_id=1, source_target_pairs={{0,1},{1,0},{2,3},{3,2},{4,5},{5,4},{6,7},{7,6},{8,9},{9,8},{10,11... | collective-permute-start | bytes 202760 | tf_op jit(solution)/shard_map/cond/branch_2_fun/ppermute | solution.py:554
  15.1 2.7 %collective-permute-start.28 = (bf16[8,4224]{1,0:T(8,128)(2,1)S(1)}, bf16[8,4224]{1,0:T(8,128)(2,1)S(1)}, u32[]{:S(2)}, u32[]{:S(2)}) collective-permute-start(bf16[8,4224]{1,0:T(8,128)(2,1)S(1)} %get-tuple-element.135.occ), channel_id=1, source_target_pairs={{0,1},{1,0},{2,3},{3,2},{4,5},{5,4},{6,7},{7,6},{8,9},{9,8},{10,11... | collective-permute-start | bytes 202760 | tf_op jit(solution)/shard_map/ppermute | solution.py:560
  19.9 1.9 %collective-permute-start.31 = (bf16[256,768]{1,0:T(8,128)(2,1)S(1)}, bf16[256,768]{1,0:T(8,128)(2,1)S(1)}, u32[]{:S(2)}, u32[]{:S(2)}) collective-permute-start(bf16[256,768]{1,0:T(8,128)(2,1)S(1)} %last.1.own), channel_id=1, source_target_pairs={{0,1},{1,0},{2,3},{3,2},{4,5},{5,4},{6,7},{7,6},{8,9},{9,8},{10,11... | collective-permute-start | bytes 1179656 | tf_op jit(solution)/shard_map/ppermute | solution.py:564
  22.2 6.2 %collective-permute-start.32 = (bf16[192,384]{1,0:T(8,128)(2,1)S(1)}, bf16[192,384]{1,0:T(8,128)(2,1)S(1)}, u32[]{:S(2)}, u32[]{:S(2)}) collective-permute-start(bf16[192,384]{1,0:T(8,128)(2,1)S(1)} %get-tuple-element.144), channel_id=1, source_target_pairs={{0,4},{1,5},{2,6},{3,7},{4,0},{5,1},{6,2},{7,3},{8,12},{9,13},{10,... | collective-permute-start | bytes 442376 | tf_op jit(solution)/shard_map/ppermute | solution.py:479
  23.8 6.7 %collective-permute-start.33 = (bf16[192,384]{1,0:T(8,128)(2,1)S(1)}, bf16[192,384]{1,0:T(8,128)(2,1)S(1)}, u32[]{:S(2)}, u32[]{:S(2)}) collective-permute-start(bf16[192,384]{1,0:T(8,128)(2,1)S(1)} %get-tuple-element.145), channel_id=1, source_target_pairs={{0,8},{1,9},{2,10},{3,11},{4,12},{5,13},{6,14},{7,15},{8,0},{9,1},... | collective-permute-start | bytes 442376 | tf_op jit(solution)/shard_map/ppermute | solution.py:479
  25.4 7.4 %collective-permute-start.34 = (bf16[192,384]{1,0:T(8,128)(2,1)S(1)}, bf16[192,384]{1,0:T(8,128)(2,1)S(1)}, u32[]{:S(2)}, u32[]{:S(2)}) collective-permute-start(bf16[192,384]{1,0:T(8,128)(2,1)S(1)} %get-tuple-element.146), channel_id=1, source_target_pairs={{0,12},{1,13},{2,14},{3,15},{4,8},{5,9},{6,10},{7,11},{8,4},{9,5},... | collective-permute-start | bytes 442376 | tf_op jit(solution)/shard_map/ppermute | solution.py:479
  33.0 4.5 %collective-permute-start.35 = (bf16[48,384]{1,0:T(8,128)(2,1)S(1)}, bf16[48,384]{1,0:T(8,128)(2,1)S(1)}, u32[]{:S(2)}, u32[]{:S(2)}) collective-permute-start(bf16[48,384]{1,0:T(8,128)(2,1)S(1)} %get-tuple-element.148), channel_id=1, source_target_pairs={{0,2},{1,3},{2,0},{3,1},{4,6},{5,7},{6,4},{7,5},{8,10},{9,11},{10,... | collective-permute-start | bytes 110600 | tf_op jit(solution)/shard_map/ppermute | solution.py:479
  34.6 5.0 %collective-permute-start.36 = (bf16[48,384]{1,0:T(8,128)(2,1)S(1)}, bf16[48,384]{1,0:T(8,128)(2,1)S(1)}, u32[]{:S(2)}, u32[]{:S(2)}) collective-permute-start(bf16[48,384]{1,0:T(8,128)(2,1)S(1)} %get-tuple-element.149), channel_id=1, source_target_pairs={{0,16},{1,17},{2,18},{3,19},{4,20},{5,21},{6,22},{7,23},{8,24},{9,... | collective-permute-start | bytes 110600 | tf_op jit(solution)/shard_map/ppermute | solution.py:479
  37.1 5.8 %collective-permute-start.37 = (bf16[48,384]{1,0:T(8,128)(2,1)S(1)}, bf16[48,384]{1,0:T(8,128)(2,1)S(1)}, u32[]{:S(2)}, u32[]{:S(2)}) collective-permute-start(bf16[48,384]{1,0:T(8,128)(2,1)S(1)} %get-tuple-element.150), channel_id=1, source_target_pairs={{0,18},{1,19},{2,16},{3,17},{4,22},{5,23},{6,20},{7,21},{8,26},{9,... | collective-permute-start | bytes 110600 | tf_op jit(solution)/shard_map/ppermute | solution.py:479

commit v2 on v1

--- a/solution.py
+++ b/solution.py
@@ -84,7 +84,7 @@
     for copy in small:
         copy.wait()
     steps = [jnp.clip(partner[moment, 0] // stride, 1, choices) - 1 for moment in range(2)]
-    choice[0, 0] = steps[0] * choices + steps[1]
+    choice[...] = jnp.full(choice.shape, steps[0] * choices + steps[1], jnp.int32)
     states = sent.shape[0]
     square = (states, states)
     here = lax.broadcasted_iota(jnp.int32, square, 0) == lax.broadcasted_iota(jnp.int32, square, 1)
@@ -102,13 +102,13 @@
     return pl.pallas_call(
         functools.partial(prepare_kernel, stride, choices),
         out_shape=[
-            jax.ShapeDtypeStruct((1, 1), jnp.int32),
+            jax.ShapeDtypeStruct((1, LANES), jnp.int32),
             half,
             half,
             jax.ShapeDtypeStruct((states, points + LANES), jnp.bfloat16),
         ],
         in_specs=[pl.BlockSpec(memory_space=pltpu.HBM)] * 4,
-        out_specs=[SMEM] + vmem(3),
+        out_specs=vmem(4),
         scratch_shapes=[
             pltpu.SMEM(partner.shape, partner.dtype),
             pltpu.VMEM(occ_energy.shape, occ_energy.dtype),

time: 43.9 us -> 43.8 us (level)
  between operations: 0.8 us -> 0.18 us
  waiting for transfers between devices: 15 us -> 15.6 us
  transfers between devices with their start and end apart: 14 -> 14, of which waited for: 7 -> 8; matrix products, arithmetic and copies ran while one was open for 3% -> 3% of each run, Pallas kernels for 8% -> 8%
where the time goes in v2:
time: 43.8 us; the launch traced here: 43.7 us
  starting transfers between devices  17.4 us (40%)
  waiting for transfers between devices  15.6 us (36%)
  Pallas kernels  8.98 us (21%)
  local copies, waits for them, and re-layouts  1.04 us (2%)
    ppermute x6, waiting for transfers between devices, exchange(): came.append(lax.ppermute(value, ('ka', 'row'), pairs))  12.7 us
    ppermute x6, starting transfers between devices, exchange(): came.append(lax.ppermute(value, ('ka', 'row'), pairs))  8.01 us
    ppermute x1, starting transfers between devices, fetch(): far = lax.ppermute(block, both, route(2))  3.4 us
    ppermute x1, starting transfers between devices, per_device(): emp_x = lax.ppermute(mine, 'row', [(i, i ^ 2) for i in range(rcount)])  3.03 us
    ppermute x1, starting transfers between devices, fetch(): near = lax.ppermute(block, both, route(0))  2.09 us
    pallas_call x1, Pallas kernels, project(): pl.pallas_call(functools.partial(last_pair_kernel, grid_x, scale), out_sh...  2.02 us
    pallas_call x1, Pallas kernels, prepare(): pl.pallas_call(functools.partial(prepare_kernel, stride, choices), out_sh...  1.8 us
    ppermute x1, waiting for transfers between devices, fetch(): far = lax.ppermute(block, both, route(2))  1.63 us
  transfers between devices with their start and end apart: 14, of which 8 were waited for; matrix products, arithmetic and copies ran while one was open for 3% of the time, Pallas kernels for 8%

profile of v2, /device:TPU:0, one launch (start us, length us, event | category | flops | bytes accessed | tf_op | source)
XLA Modules:
  0.0 43.7 jit_solution(9981061487982932795)
XLA Ops:
  0.0 1.8 %prepare.1 = (s32[1,128]{1,0:T(1,128)S(1)}, bf16[32,4096]{1,0:T(8,128)(2,1)S(1)}, bf16[32,4096]{1,0:T(8,128)(2,1)}, bf16[8,4224]{1,0:T(8,128)(2,1)S(1)}) custom-call(s32[2,8]{1,0:T(2,128)} %table.1, bf16[1,8]{1,0:T(2,128)(2,1)} %energy.2, bf16[1,64,4096]{2,1,0:T(8,128)(2,1)} %empty.1, bf16[1,8,4096]{2,1,0:T(8,128)(2,1)} %occupied.1), custom_call_target="tpu_custom_call" | custom-call | tf_op jit(solution)/shard_map/prepare/pallas_call | solution.py:102
  1.8 3.0 %collective-permute-start.30 = (bf16[32,4096]{1,0:T(8,128)(2,1)S(1)}, bf16[32,4096]{1,0:T(8,128)(2,1)S(1)}, u32[]{:S(2)}, u32[]{:S(2)}) collective-permute-start(bf16[32,4096]{1,0:T(8,128)(2,1)S(1)} %get-tuple-element.137.emp), channel_id=1, source_target_pairs={{0,2},{1,3},{2,0},{3,1},{4,6},{5,7},{6,4},{7,5},{8,10},{9,11},{10,... | collective-permute-start | bytes 786440 | tf_op jit(solution)/shard_map/ppermute | solution.py:534
  5.1 9.4 %conditional.1 = (bf16[8,4224]{1,0:T(8,128)(2,1)S(1)}, bf16[8,4224]{1,0:T(8,128)(2,1)S(1)}, bf16[8,4224]{1,0:T(8,128)(2,1)S(1)}, bf16[1152,768]{1,0:T(8,128)(2,1)S(1)}) conditional(s32[]{:T(128)} %bitcast.135, (bf16[8,4224]{1,0:T(8,128)(2,1)S(1)}, s32[]{:T(128)}, s32[2,384,3]{1,0,2:T(2,128)}) %tuple.41, ...), branch_computations={%region_0.1_spmd, %region_1.2_spmd, %region_2.3_spmd, %region_3.4_... | conditional | flops 26115 | bytes 954050 | solution.py:559
  5.1 2.1 %collective-permute-start.6 = (bf16[8,4224]{1,0:T(8,128)(2,1)S(1)}, bf16[8,4224]{1,0:T(8,128)(2,1)S(1)}, u32[]{:S(2)}, u32[]{:S(2)}) collective-permute-start(bf16[8,4224]{1,0:T(8,128)(2,1)S(1)} %get-tuple-element.71), channel_id=1, source_target_pairs={{0,8},{1,9},{2,26},{3,27},{4,12},{5,13},{6,30},{7,31},{8,16},{9,17... | collective-permute-start | bytes 202760 | tf_op jit(solution)/shard_map/cond/branch_2_fun/ppermute | solution.py:553
  7.2 3.4 %collective-permute-start.8 = (bf16[8,4224]{1,0:T(8,128)(2,1)S(1)}, bf16[8,4224]{1,0:T(8,128)(2,1)S(1)}, u32[]{:S(2)}, u32[]{:S(2)}) collective-permute-start(bf16[8,4224]{1,0:T(8,128)(2,1)S(1)} %get-tuple-element.71), channel_id=1, source_target_pairs={{0,26},{1,27},{2,8},{3,9},{4,30},{5,31},{6,12},{7,13},{8,2},{9,3},... | collective-permute-start | bytes 202760 | tf_op jit(solution)/shard_map/cond/branch_2_fun/ppermute | solution.py:552
  10.6 0.7 %copy.10 = s32[2,384,3]{1,2,0:T(4,128)S(1)} copy(s32[2,384,3]{1,0,2:T(2,128)} %get-tuple-element.159) | data formatting | bytes 18432 | tf_op jit(solution)/shard_map
  12.1 0.7 %matrix.11 = bf16[1152,768]{1,0:T(8,128)(2,1)S(1)} custom-call(s32[4,768]{1,0:T(4,128)S(1)} %pad_add_fusion.10.index), custom_call_target="tpu_custom_call" | custom-call | tf_op jit(solution)/shard_map/cond/branch_2_fun/matrix/pallas_call | solution.py:257
  12.8 1.6 %collective-permute-done.8.refs_2_ = bf16[8,4224]{1,0:T(8,128)(2,1)S(1)} collective-permute-done((bf16[8,4224]{1,0:T(8,128)(2,1)S(1)}, bf16[8,4224]{1,0:T(8,128)(2,1)S(1)}, u32[]{:S(2)}, u32[]{:S(2)}) %collective-permute-start.8) | collective-permute-done | bytes 67616 | tf_op jit(solution)/shard_map/cond/branch_2_fun/ppermute | solution.py:552
  14.6 0.7 %shard_map.74 = (f32[8,256,128]{2,1,0:T(8,128)S(1)}, f32[256,128]{1,0:T(8,128)S(1)}, f32[256,128]{1,0:T(8,128)S(1)}) custom-call(bf16[32,4096]{1,0:T(8,128)(2,1)S(1)} %get-tuple-element.137.emp, bf16[8,4224]{1,0:T(8,128)(2,1)S(1)} %get-tuple-element.138.occ, bf16[512,256]{1,0:T(8,128)(2,1)S(1)} %copy-done, bf16[1,64]{1,0:T(2,128)(2,1)S(1)} %copy-done.1), custom_call_target="tpu_custom_call" | custom-call | tf_op jit(solution)/shard_map/pallas_call | solution.py:359
  15.3 1.2 %pair.1.before = f32[9,256,128]{2,1,0:T(8,128)S(1)} custom-call(bf16[32,4096]{1,0:T(8,128)(2,1)S(1)} %collective-permute-done.30.emp, bf16[8,4224]{1,0:T(8,128)(2,1)S(1)} %get-tuple-element.135.occ, bf16[512,256]{1,0:T(8,128)(2,1)S(1)} %copy-done, f32[8,256,128]{2,1,0:T(8,128)S(1)} %get-tuple-element.139.near), custom_call_target="tpu_custom_call" | custom-call | tf_op jit(solution)/shard_map/pair/pallas_call | solution.py:371
  16.5 0.7 %shard_map.73.near = f32[8,256,128]{2,1,0:T(8,128)S(1)} custom-call(bf16[32,4096]{1,0:T(8,128)(2,1)S(1)} %collective-permute-done.29.emp, bf16[8,4224]{1,0:T(8,128)(2,1)S(1)} %get-tuple-element.136.occ, bf16[512,256]{1,0:T(8,128)(2,1)S(1)} %copy-done), custom_call_target="tpu_custom_call" | custom-call | tf_op jit(solution)/shard_map/pallas_call | solution.py:359
  17.6 2.0 %last.1.own = bf16[256,768]{1,0:T(8,128)(2,1)S(1)} custom-call(bf16[32,4096]{1,0:T(8,128)(2,1)S(1)} %collective-permute-done.27.emp, bf16[8,4224]{1,0:T(8,128)(2,1)S(1)} %collective-permute-done.28.occ, bf16[512,256]{1,0:T(8,128)(2,1)S(1)} %copy-done, f32[8,256,128]{2,1,0:T(8,128)S(1)} %shard_map.73.near, f32[9,256,128]{2,1,0:T(8,128)S(1)} %pair.1.before, ...), custom_call_target="tpu_custom_call" | custom-call | tf_op jit(solution)/shard_map/last/pallas_call | solution.py:380
  19.6 0.5 %collective-permute-start.31 = (bf16[256,768]{1,0:T(8,128)(2,1)S(1)}, bf16[256,768]{1,0:T(8,128)(2,1)S(1)}, u32[]{:S(2)}, u32[]{:S(2)}) collective-permute-start(bf16[256,768]{1,0:T(8,128)(2,1)S(1)} %last.1.own), channel_id=1, source_target_pairs={{0,1},{1,0},{2,3},{3,2},{4,5},{5,4},{6,7},{7,6},{8,9},{9,8},{10,11... | collective-permute-start | bytes 1179656 | tf_op jit(solution)/shard_map/ppermute | solution.py:564
  20.5 1.0 %collective-permute-done.31.other = bf16[256,768]{1,0:T(8,128)(2,1)S(1)} collective-permute-done((bf16[256,768]{1,0:T(8,128)(2,1)S(1)}, bf16[256,768]{1,0:T(8,128)(2,1)S(1)}, u32[]{:S(2)}, u32[]{:S(2)}) %collective-permute-start.31) | collective-permute-done | bytes 393248 | tf_op jit(solution)/shard_map/ppermute | solution.py:564
  21.9 1.8 %collective-permute-start.32 = (bf16[192,384]{1,0:T(8,128)(2,1)S(1)}, bf16[192,384]{1,0:T(8,128)(2,1)S(1)}, u32[]{:S(2)}, u32[]{:S(2)}) collective-permute-start(bf16[192,384]{1,0:T(8,128)(2,1)S(1)} %get-tuple-element.144), channel_id=1, source_target_pairs={{0,4},{1,5},{2,6},{3,7},{4,0},{5,1},{6,2},{7,3},{8,12},{9,13},{10,... | collective-permute-start | bytes 442376 | tf_op jit(solution)/shard_map/ppermute | solution.py:479
  23.8 1.6 %collective-permute-start.33 = (bf16[192,384]{1,0:T(8,128)(2,1)S(1)}, bf16[192,384]{1,0:T(8,128)(2,1)S(1)}, u32[]{:S(2)}, u32[]{:S(2)}) collective-permute-start(bf16[192,384]{1,0:T(8,128)(2,1)S(1)} %get-tuple-element.145), channel_id=1, source_target_pairs={{0,8},{1,9},{2,10},{3,11},{4,12},{5,13},{6,14},{7,15},{8,0},{9,1},... | collective-permute-start | bytes 442376 | tf_op jit(solution)/shard_map/ppermute | solution.py:479
  25.5 2.7 %collective-permute-done.32.from_y = bf16[192,384]{1,0:T(8,128)(2,1)S(1)} collective-permute-done((bf16[192,384]{1,0:T(8,128)(2,1)S(1)}, bf16[192,384]{1,0:T(8,128)(2,1)S(1)}, u32[]{:S(2)}, u32[]{:S(2)}) %collective-permute-start.32) | collective-permute-done | bytes 147488 | tf_op jit(solution)/shard_map/ppermute | solution.py:479
  28.2 2.3 %collective-permute-done.33.from_z = bf16[192,384]{1,0:T(8,128)(2,1)S(1)} collective-permute-done((bf16[192,384]{1,0:T(8,128)(2,1)S(1)}, bf16[192,384]{1,0:T(8,128)(2,1)S(1)}, u32[]{:S(2)}, u32[]{:S(2)}) %collective-permute-start.33) | collective-permute-done | bytes 147488 | tf_op jit(solution)/shard_map/ppermute | solution.py:479
  30.5 2.1 %collective-permute-done.34.from_yz = bf16[192,384]{1,0:T(8,128)(2,1)S(1)} collective-permute-done((bf16[192,384]{1,0:T(8,128)(2,1)S(1)}, bf16[192,384]{1,0:T(8,128)(2,1)S(1)}, u32[]{:S(2)}, u32[]{:S(2)}) %collective-permute-start.34) | collective-permute-done | bytes 147488 | tf_op jit(solution)/shard_map/ppermute | solution.py:479
  32.8 1.7 %collective-permute-start.35 = (bf16[48,384]{1,0:T(8,128)(2,1)S(1)}, bf16[48,384]{1,0:T(8,128)(2,1)S(1)}, u32[]{:S(2)}, u32[]{:S(2)}) collective-permute-start(bf16[48,384]{1,0:T(8,128)(2,1)S(1)} %get-tuple-element.148), channel_id=1, source_target_pairs={{0,2},{1,3},{2,0},{3,1},{4,6},{5,7},{6,4},{7,5},{8,10},{9,11},{10,... | collective-permute-start | bytes 110600 | tf_op jit(solution)/shard_map/ppermute | solution.py:479
  34.5 2.6 %collective-permute-start.36 = (bf16[48,384]{1,0:T(8,128)(2,1)S(1)}, bf16[48,384]{1,0:T(8,128)(2,1)S(1)}, u32[]{:S(2)}, u32[]{:S(2)}) collective-permute-start(bf16[48,384]{1,0:T(8,128)(2,1)S(1)} %get-tuple-element.149), channel_id=1, source_target_pairs={{0,16},{1,17},{2,18},{3,19},{4,20},{5,21},{6,22},{7,23},{8,24},{9,... | collective-permute-start | bytes 110600 | tf_op jit(solution)/shard_map/ppermute | solution.py:479
  37.3 2.2 %collective-permute-done.36.from_z = bf16[48,384]{1,0:T(8,128)(2,1)S(1)} collective-permute-done((bf16[48,384]{1,0:T(8,128)(2,1)S(1)}, bf16[48,384]{1,0:T(8,128)(2,1)S(1)}, u32[]{:S(2)}, u32[]{:S(2)}) %collective-permute-start.36) | collective-permute-done | bytes 36896 | tf_op jit(solution)/shard_map/ppermute | solution.py:479
  39.5 3.4 %collective-permute-done.37.from_xz = bf16[48,384]{1,0:T(8,128)(2,1)S(1)} collective-permute-done((bf16[48,384]{1,0:T(8,128)(2,1)S(1)}, bf16[48,384]{1,0:T(8,128)(2,1)S(1)}, u32[]{:S(2)}, u32[]{:S(2)}) %collective-permute-start.37) | collective-permute-done | bytes 36896 | tf_op jit(solution)/shard_map/ppermute | solution.py:479
  42.9 0.8 %final.1 = f32[2,96,192]{2,1,0:T(8,128)} custom-call(f32[48,384]{1,0:T(8,128)S(1)} %get-tuple-element.147.stay, bf16[48,384]{1,0:T(8,128)(2,1)S(1)} %collective-permute-done.35.from_x, bf16[48,384]{1,0:T(8,128)(2,1)S(1)} %collective-permute-done.36.from_z, bf16[48,384]{1,0:T(8,128)(2,1)S(1)} %collective-permute-done.37.from_xz), custom_call_target="tpu_custom_call" | custom-call | tf_op jit(solution)/shard_map/final/pallas_call | solution.py:494
  (38 shorter events, 2.8 us)
Async XLA Ops:
  1.8 13.5 %collective-permute-start.30 = (bf16[32,4096]{1,0:T(8,128)(2,1)S(1)}, bf16[32,4096]{1,0:T(8,128)(2,1)S(1)}, u32[]{:S(2)}, u32[]{:S(2)}) collective-permute-start(bf16[32,4096]{1,0:T(8,128)(2,1)S(1)} %get-tuple-element.137.emp), channel_id=1, source_target_pairs={{0,2},{1,3},{2,0},{3,1},{4,6},{5,7},{6,4},{7,5},{8,10},{9,11},{10,... | collective-permute-start | bytes 786440 | tf_op jit(solution)/shard_map/ppermute | solution.py:534
  4.8 11.6 %collective-permute-start.29 = (bf16[32,4096]{1,0:T(8,128)(2,1)}, bf16[32,4096]{1,0:T(8,128)(2,1)S(1)}, u32[]{:S(2)}, u32[]{:S(2)}) collective-permute-start(bf16[32,4096]{1,0:T(8,128)(2,1)} %get-tuple-element.132), channel_id=1, source_target_pairs={{0,1},{1,0},{2,3},{3,2},{4,5},{5,4},{6,7},{7,6},{8,9},{9,8},{10,11... | collective-permute-start | bytes 786440 | tf_op jit(solution)/shard_map/ppermute | solution.py:536
  4.8 12.7 %collective-permute-start.27 = (bf16[32,4096]{1,0:T(8,128)(2,1)}, bf16[32,4096]{1,0:T(8,128)(2,1)S(1)}, u32[]{:S(2)}, u32[]{:S(2)}) collective-permute-start(bf16[32,4096]{1,0:T(8,128)(2,1)} %get-tuple-element.132), channel_id=1, source_target_pairs={{0,3},{1,2},{2,1},{3,0},{4,7},{5,6},{6,5},{7,4},{8,11},{9,10},{10,... | collective-permute-start | bytes 786440 | tf_op jit(solution)/shard_map/ppermute | solution.py:535
  5.1 9.5 %copy-start = (bf16[512,256]{1,0:T(8,128)(2,1)S(1)}, bf16[512,256]{1,0:T(8,128)(2,1)}, u32[]{:S(2)}) copy-start(bf16[512,256]{1,0:T(8,128)(2,1)} %constant.199.clone.plane) | copy-start | bytes 786436
  5.1 9.5 %copy-start.1 = (bf16[1,64]{1,0:T(2,128)(2,1)S(1)}, bf16[1,64]{1,0:T(2,128)(2,1)}, u32[]{:S(2)}) copy-start(bf16[1,64]{1,0:T(2,128)(2,1)} %energy.3) | copy-start | bytes 388
  5.1 6.9 %collective-permute-start.6 = (bf16[8,4224]{1,0:T(8,128)(2,1)S(1)}, bf16[8,4224]{1,0:T(8,128)(2,1)S(1)}, u32[]{:S(2)}, u32[]{:S(2)}) collective-permute-start(bf16[8,4224]{1,0:T(8,128)(2,1)S(1)} %get-tuple-element.71), channel_id=1, source_target_pairs={{0,8},{1,9},{2,26},{3,27},{4,12},{5,13},{6,30},{7,31},{8,16},{9,17... | collective-permute-start | bytes 202760 | tf_op jit(solution)/shard_map/cond/branch_2_fun/ppermute | solution.py:553
  7.2 7.2 %collective-permute-start.8 = (bf16[8,4224]{1,0:T(8,128)(2,1)S(1)}, bf16[8,4224]{1,0:T(8,128)(2,1)S(1)}, u32[]{:S(2)}, u32[]{:S(2)}) collective-permute-start(bf16[8,4224]{1,0:T(8,128)(2,1)S(1)} %get-tuple-element.71), channel_id=1, source_target_pairs={{0,26},{1,27},{2,8},{3,9},{4,30},{5,31},{6,12},{7,13},{8,2},{9,3},... | collective-permute-start | bytes 202760 | tf_op jit(solution)/shard_map/cond/branch_2_fun/ppermute | solution.py:552
  12.0 2.4 %collective-permute-start.7 = (bf16[8,4224]{1,0:T(8,128)(2,1)S(1)}, bf16[8,4224]{1,0:T(8,128)(2,1)S(1)}, u32[]{:S(2)}, u32[]{:S(2)}) collective-permute-start(bf16[8,4224]{1,0:T(8,128)(2,1)S(1)} %collective-permute-done.6.refs_0_), channel_id=1, source_target_pairs={{0,1},{1,0},{2,3},{3,2},{4,5},{5,4},{6,7},{7,6},{8,9},{9,8},{10,11... | collective-permute-start | bytes 202760 | tf_op jit(solution)/shard_map/cond/branch_2_fun/ppermute | solution.py:554
  14.5 2.7 %collective-permute-start.28 = (bf16[8,4224]{1,0:T(8,128)(2,1)S(1)}, bf16[8,4224]{1,0:T(8,128)(2,1)S(1)}, u32[]{:S(2)}, u32[]{:S(2)}) collective-permute-start(bf16[8,4224]{1,0:T(8,128)(2,1)S(1)} %get-tuple-element.135.occ), channel_id=1, source_target_pairs={{0,1},{1,0},{2,3},{3,2},{4,5},{5,4},{6,7},{7,6},{8,9},{9,8},{10,11... | collective-permute-start | bytes 202760 | tf_op jit(solution)/shard_map/ppermute | solution.py:560
  19.6 1.9 %collective-permute-start.31 = (bf16[256,768]{1,0:T(8,128)(2,1)S(1)}, bf16[256,768]{1,0:T(8,128)(2,1)S(1)}, u32[]{:S(2)}, u32[]{:S(2)}) collective-permute-start(bf16[256,768]{1,0:T(8,128)(2,1)S(1)} %last.1.own), channel_id=1, source_target_pairs={{0,1},{1,0},{2,3},{3,2},{4,5},{5,4},{6,7},{7,6},{8,9},{9,8},{10,11... | collective-permute-start | bytes 1179656 | tf_op jit(solution)/shard_map/ppermute | solution.py:564
  21.9 6.2 %collective-permute-start.32 = (bf16[192,384]{1,0:T(8,128)(2,1)S(1)}, bf16[192,384]{1,0:T(8,128)(2,1)S(1)}, u32[]{:S(2)}, u32[]{:S(2)}) collective-permute-start(bf16[192,384]{1,0:T(8,128)(2,1)S(1)} %get-tuple-element.144), channel_id=1, source_target_pairs={{0,4},{1,5},{2,6},{3,7},{4,0},{5,1},{6,2},{7,3},{8,12},{9,13},{10,... | collective-permute-start | bytes 442376 | tf_op jit(solution)/shard_map/ppermute | solution.py:479
  23.8 6.7 %collective-permute-start.33 = (bf16[192,384]{1,0:T(8,128)(2,1)S(1)}, bf16[192,384]{1,0:T(8,128)(2,1)S(1)}, u32[]{:S(2)}, u32[]{:S(2)}) collective-permute-start(bf16[192,384]{1,0:T(8,128)(2,1)S(1)} %get-tuple-element.145), channel_id=1, source_target_pairs={{0,8},{1,9},{2,10},{3,11},{4,12},{5,13},{6,14},{7,15},{8,0},{9,1},... | collective-permute-start | bytes 442376 | tf_op jit(solution)/shard_map/ppermute | solution.py:479
  25.4 7.2 %collective-permute-start.34 = (bf16[192,384]{1,0:T(8,128)(2,1)S(1)}, bf16[192,384]{1,0:T(8,128)(2,1)S(1)}, u32[]{:S(2)}, u32[]{:S(2)}) collective-permute-start(bf16[192,384]{1,0:T(8,128)(2,1)S(1)} %get-tuple-element.146), channel_id=1, source_target_pairs={{0,12},{1,13},{2,14},{3,15},{4,8},{5,9},{6,10},{7,11},{8,4},{9,5},... | collective-permute-start | bytes 442376 | tf_op jit(solution)/shard_map/ppermute | solution.py:479
  32.8 4.5 %collective-permute-start.35 = (bf16[48,384]{1,0:T(8,128)(2,1)S(1)}, bf16[48,384]{1,0:T(8,128)(2,1)S(1)}, u32[]{:S(2)}, u32[]{:S(2)}) collective-permute-start(bf16[48,384]{1,0:T(8,128)(2,1)S(1)} %get-tuple-element.148), channel_id=1, source_target_pairs={{0,2},{1,3},{2,0},{3,1},{4,6},{5,7},{6,4},{7,5},{8,10},{9,11},{10,... | collective-permute-start | bytes 110600 | tf_op jit(solution)/shard_map/ppermute | solution.py:479
  34.5 5.0 %collective-permute-start.36 = (bf16[48,384]{1,0:T(8,128)(2,1)S(1)}, bf16[48,384]{1,0:T(8,128)(2,1)S(1)}, u32[]{:S(2)}, u32[]{:S(2)}) collective-permute-start(bf16[48,384]{1,0:T(8,128)(2,1)S(1)} %get-tuple-element.149), channel_id=1, source_target_pairs={{0,16},{1,17},{2,18},{3,19},{4,20},{5,21},{6,22},{7,23},{8,24},{9,... | collective-permute-start | bytes 110600 | tf_op jit(solution)/shard_map/ppermute | solution.py:479
  37.1 5.8 %collective-permute-start.37 = (bf16[48,384]{1,0:T(8,128)(2,1)S(1)}, bf16[48,384]{1,0:T(8,128)(2,1)S(1)}, u32[]{:S(2)}, u32[]{:S(2)}) collective-permute-start(bf16[48,384]{1,0:T(8,128)(2,1)S(1)} %get-tuple-element.150), channel_id=1, source_target_pairs={{0,18},{1,19},{2,16},{3,17},{4,22},{5,23},{6,20},{7,21},{8,26},{9,... | collective-permute-start | bytes 110600 | tf_op jit(solution)/shard_map/ppermute | solution.py:479
